TPU v7x, 256 devices: a whole 4x4x8 slice. The times are simulated.
256 devices in a mesh: wide: 16 (over x, y), perm: 16 (over z, core).
Axes of the slice: x: 4, y: 4, z: 8, core: 2. Of those that a mesh axis runs over, the one named last changes fastest.
Arguments:
- amplitudes: bfloat16 [64, 2048, 2048], P('wide', 'perm'), may hold values from -6 to 6
- integrals: bfloat16 [2048, 2048], P('perm'), may hold values from -0.125 to 0.125
- coupling: float32 [64, 9], replicated, may hold values from -2 to 2
- pair_energy: float32 [64], P('wide'), may hold values from -2 to -0.5
- virtual_energy: float32 [2048], replicated, may hold values from 0.5 to 3
- tile_sizes: int32 [16], replicated, may hold values from 64 to 128, as said below
- blocks: int32 [64, 16, 16], P('wide'), may hold values 0 or 1
Outputs:
- update: bfloat16 [64, 2048, 2048], P('wide', 'perm')
Inputs may be any that keep to these rules, and one draw needn't show every extreme that they name: `tile_sizes`: some tile has 128 live slots and some tile 128 // 2.
All inputs are finite; a program needn't handle non-finite values. No bound on the sum of `blocks` on one device may be relied on, other than what follows from the above.
Results may differ from a plain program's by a relative error of at most 0.0058.
Values may be sent and summed in bfloat16 or wider, within the bound.
No kernel may reach another device: no remote copies, remote signals or barrier semaphores. Data moves between devices by JAX's collectives and lax.ppermute only.
A program may use at most 128 MiB of HBM per device.

v0:
```python
import functools

import jax
import jax.numpy as jnp
from jax import lax
from jax.experimental import pallas as pl
from jax.experimental.pallas import tpu as pltpu
from jax.sharding import PartitionSpec as P


TILE = 128
PARTS = 2
STREAMS = 4
EARLY = (3, 4)
LATE = (5, 2, 6, 1, 7)
FINISH = ((0, 4, 3, 5), (2, 6, 1, 7))


def wide_shift(block, distance):
    size = lax.axis_size("wide")
    route = [(i, i + distance) for i in range(size) if 0 <= i + distance < size]
    return lax.ppermute(block, "wide", route)


def core_swap(block):
    size = lax.axis_size("perm")
    return lax.ppermute(block, "perm", [(i, i ^ 1) for i in range(size)])


def mirrored(block, distance):
    size = lax.axis_size("perm")
    chips = size // 2
    route = []
    for i in range(size):
        z, core = divmod(i, 2)
        route.append((i, (z + (distance if core == 0 else -distance)) % chips * 2 + core))
    return lax.ppermute(block, "perm", route)


def place():
    index = lax.axis_index("perm")
    return index // 2, lax.rem(index, 2)


def steps_from(z, chips, turn=0):
    own, core = place()
    core = lax.rem(core + turn, 2)
    ahead = lax.rem(own - z + chips, chips)
    return jnp.where(core == 0, ahead, lax.rem(chips - ahead, chips))


def mix_body(coef_ref, before_ref, own_ref, after_ref, *mixed_refs):
    pairs, rows, width = own_ref.shape
    taps = coef_ref.shape[1]
    chips = width // TILE // 2
    step = 32

    def one_tile(t, carry):
        source = pl.ds(pl.multiple_of(t * TILE, TILE), TILE)
        targets = []
        for turn in range(2):
            dz = steps_from(t // 2, chips, turn)
            dc = lax.rem(t + place()[1] + turn, 2)
            targets.append(pl.ds(pl.multiple_of((dz * 2 + dc) * TILE, TILE), TILE))
        for start in range(0, rows, step):
            total = [None] * pairs
            for q in range(3 * pairs):
                ref = (before_ref, own_ref, after_ref)[q // pairs]
                value = ref[q % pairs, start : start + step, source].astype(jnp.float32)
                for p in range(pairs):
                    if 0 <= q - p < taps:
                        term = coef_ref[p, q - p] * value
                        total[p] = term if total[p] is None else total[p] + term
            for p in range(pairs):
                rounded = total[p].astype(jnp.bfloat16)
                for ref, target in zip(mixed_refs, targets):
                    ref[p, start : start + step, target] = rounded
        return carry

    lax.fori_loop(0, width // TILE, one_tile, 0)


def mix(which, coef, before, own, after):
    pairs, rows, width = own.shape
    rows = rows // PARTS
    step = 32
    smem = pl.BlockSpec(memory_space=pltpu.SMEM)
    skip = which * rows // step
    spec = pl.BlockSpec((pairs, step, width), lambda t: (0, skip + t, 0))
    return pl.pallas_call(
        mix_body,
        out_shape=[jax.ShapeDtypeStruct((pairs, rows, width), jnp.bfloat16)] * 2,
        grid=(rows // step,),
        in_specs=[smem, spec, spec, spec],
        out_specs=[pl.BlockSpec((pairs, step, width), lambda t: (0, t, 0))] * 2,
        cost_estimate=pl.CostEstimate(
            flops=18 * pairs * rows * width, bytes_accessed=8 * pairs * rows * width, transcendentals=0
        ),
        name="mix",
    )(coef, before, own, after)


def split_body(in_ref, *refs):
    kept_refs, given_ref = refs[:-1], refs[-1]
    depth = kept_refs[0].shape[0]
    _, core = place()
    for z in range(given_ref.shape[1] // TILE):
        target = pl.ds(z * TILE, TILE)
        mine = pl.ds(pl.multiple_of((2 * z + core) * TILE, TILE), TILE)
        other = pl.ds(pl.multiple_of((2 * z + 1 - core) * TILE, TILE), TILE)
        given_ref[:, target] = in_ref[:, other]
        for i, ref in enumerate(kept_refs):
            ref[:, target] = in_ref[i * depth : (i + 1) * depth, mine]


def split(integrals):
    rows, width = integrals.shape
    depth = 2 * rows // STREAMS
    count = rows // depth
    vmem = pl.BlockSpec(memory_space=pltpu.VMEM)
    return pl.pallas_call(
        split_body,
        out_shape=[jax.ShapeDtypeStruct((depth, width // 2), jnp.bfloat16)] * count
        + [jax.ShapeDtypeStruct((rows, width // 2), jnp.bfloat16)],
        in_specs=[vmem],
        out_specs=[vmem] * (count + 1),
        cost_estimate=pl.CostEstimate(flops=0, bytes_accessed=4 * rows * width, transcendentals=0),
        name="split",
    )(integrals)


def product_body(count, chips, *refs):
    mixed_refs, pieces, outs = refs[:2], refs[2 : 2 + count], refs[-2 - chips :]
    own_refs, sent_refs = outs[:2], outs[2:]
    pairs, rows, width = mixed_refs[0].shape
    halves = sent_refs[0].shape[2]
    weights = jnp.concatenate([piece[...] for piece in pieces], axis=0)
    left = jnp.concatenate([ref[...].reshape(pairs * rows, width) for ref in mixed_refs], axis=0)
    result = jnp.dot(left, weights, preferred_element_type=jnp.float32).astype(jnp.bfloat16)
    for c in range(2):
        part = result[c * pairs * rows : (c + 1) * pairs * rows]
        own_refs[c][...] = part.reshape(pairs, rows, part.shape[1])
    turned = result.T
    group = result.shape[1] // TILE
    for i in range(group):
        z = pl.program_id(0) * group + i
        slot = lax.rem(chips - steps_from(z, chips), chips)

        def store(ref, i=i):
            for c in range(2):
                for h in range(halves):
                    start = (c * halves + h) * TILE
                    ref[0, c, h] = turned[i * TILE : (i + 1) * TILE, start : start + TILE]

        for d in range(chips):
            pl.when(slot == d)(functools.partial(store, sent_refs[d]))


def product(which, mixed, other, pieces, own_targets, sent_targets):
    pairs, rows, width = mixed.shape
    columns = pieces[0].shape[1]
    chips = columns // TILE
    wide = 2 * TILE
    halves = pairs * rows // TILE
    own = jax.ShapeDtypeStruct((pairs, PARTS * rows, columns), jnp.bfloat16)
    own_spec = pl.BlockSpec((pairs, rows, wide), lambda t: (0, which, t))
    inner = (2, halves, TILE, TILE)
    sent_shapes, sent_specs = [], []
    targets = list(own_targets)
    aliases = {2 + len(pieces) + i: i for i in range(len(targets))}
    for d in range(chips):
        apart = d in EARLY
        sent_shapes.append(jax.ShapeDtypeStruct((1 if apart else PARTS,) + inner, jnp.bfloat16))
        at = 0 if apart else which
        sent_specs.append(pl.BlockSpec((1,) + inner, lambda t, at=at: (at, 0, 0, 0, 0)))
        if sent_targets and not apart:
            aliases[2 + len(pieces) + len(targets)] = 2 + d
            targets.append(sent_targets[d])
    return pl.pallas_call(
        functools.partial(product_body, len(pieces), chips),
        out_shape=[own, own] + sent_shapes,
        grid=(columns // wide,),
        in_specs=[pl.BlockSpec((pairs, rows, width), lambda t: (0, 0, 0))] * 2
        + [pl.BlockSpec((piece.shape[0], wide), lambda t: (0, t)) for piece in pieces]
        + [pl.BlockSpec(memory_space=pl.ANY)] * len(targets),
        out_specs=[own_spec, own_spec] + sent_specs,
        input_output_aliases=aliases,
        cost_estimate=pl.CostEstimate(
            flops=4 * pairs * rows * width * columns,
            bytes_accessed=4 * pairs * rows * (width + columns) + 2 * width * columns,
            transcendentals=0,
        ),
        name="product",
    )(mixed, other, *pieces, *targets)


def finish_body(splits, source_ref, sizes_ref, pair_ref, block_ref, row_ref, column_ref, own_ref, other_ref, *refs):
    out_ref = refs[-1]
    pairs = out_ref.shape[0]
    halves = refs[0].shape[2]
    share = pairs // halves
    inner = TILE // share
    own, core = place()
    shape = (TILE, TILE)
    row_live = lax.broadcasted_iota(jnp.int32, shape, 0) < sizes_ref[own * 2 + core]
    lane = lax.broadcasted_iota(jnp.int32, shape, 1)
    source = source_ref[pl.program_id(0)]

    def one(blocks):
        for rel, mine_ref in enumerate((own_ref, other_ref)):
            half = lax.rem(core + rel, 2)
            tile = source * 2 + half
            target = pl.ds(pl.multiple_of(half * TILE, TILE), TILE)
            live = row_live & (lane < sizes_ref[tile])
            energy = row_ref[...] + column_ref[half]

            def some_pairs(h, carry):
                for i in range(share):
                    p = h * share + i
                    theirs = jnp.concatenate(
                        [ref[r, rel, h, :, i * inner : (i + 1) * inner] for ref, r in blocks], axis=1
                    )
                    residual = mine_ref[p].astype(jnp.float32) + theirs.astype(jnp.float32)
                    block = jnp.where(live, block_ref[tile, p].astype(jnp.float32), 0.0)
                    scaled = residual * pl.reciprocal(energy - pair_ref[p])
                    out_ref[p, :, target] = (block * scaled).astype(jnp.bfloat16)
                return carry

            lax.fori_loop(0, halves, some_pairs, 0)

    first = 0
    for d, count in enumerate(splits):
        if count == 1:
            blocks = [(refs[first], r) for r in range(PARTS)]
        else:
            blocks = [(refs[first + r], 0) for r in range(PARTS)]
        pl.when(pl.program_id(0) == d)(functools.partial(one, blocks))
        first += count


def finish(sources, sizes, pair_energy, block_row, energy_row, energy_all, own, other, arrived, target):
    pairs, rows, columns = own.shape
    count = len(arrived)
    splits = tuple(len(blocks) for blocks in arrived)
    swapped = [block for blocks in arrived for block in blocks]
    smem = pl.BlockSpec(memory_space=pltpu.SMEM)
    own_spec = pl.BlockSpec((pairs, rows, TILE), lambda t, source: (0, 0, source[t]))
    before = 8 + len(swapped)
    return pl.pallas_call(
        functools.partial(finish_body, splits),
        out_shape=jax.ShapeDtypeStruct((pairs, rows, 2 * columns), jnp.bfloat16),
        grid_spec=pltpu.PrefetchScalarGridSpec(
            num_scalar_prefetch=1,
            grid=(count,),
            in_specs=[
                smem,
                smem,
                smem,
                pl.BlockSpec((rows, 1), lambda t, source: (0, 0)),
                pl.BlockSpec((2, 1, TILE), lambda t, source: (source[t], 0, 0)),
                own_spec,
                own_spec,
            ]
            + [pl.BlockSpec(block.shape, lambda t, source: (0, 0, 0, 0, 0)) for block in swapped]
            + ([] if target is None else [pl.BlockSpec(memory_space=pl.ANY)]),
            out_specs=pl.BlockSpec((pairs, rows, 2 * TILE), lambda t, source: (0, 0, source[t])),
        ),
        input_output_aliases={} if target is None else {before: 0},
        cost_estimate=pl.CostEstimate(
            flops=20 * count * pairs * rows * TILE,
            bytes_accessed=12 * count * pairs * rows * TILE,
            transcendentals=0,
        ),
        name="finish",
    )(
        sources,
        sizes,
        pair_energy,
        block_row,
        energy_row,
        energy_all,
        own,
        other,
        *swapped,
        *([] if target is None else [target]),
    )


def per_device(amplitudes, integrals, coupling, pair_energy, virtual_energy, tile_sizes, blocks):
    pairs, rows, _ = amplitudes.shape
    tiles = tile_sizes.shape[0]
    chips = tiles // 2
    wide_index = lax.axis_index("wide")
    perm_index = lax.axis_index("perm")
    coef = lax.dynamic_slice_in_dim(coupling, wide_index * pairs, pairs, 0)
    before = wide_shift(amplitudes, 1)
    after = wide_shift(amplitudes, -1)
    *kept_columns, given_columns = split(integrals)
    taken_columns = core_swap(given_columns)
    depth = 2 * rows // STREAMS
    moving = kept_columns + [taken_columns[start : start + depth] for start in range(0, rows, depth)]
    pieces = list(moving)
    for _ in range(1, chips):
        for i in range(STREAMS):
            moving[i] = mirrored(moving[i], 1)
        pieces += moving
    mixed, other = [], []
    for r in range(PARTS):
        kept_rows, given_rows = mix(r, coef, before, amplitudes, after)
        mixed.append(kept_rows)
        other.append(core_swap(given_rows))
    own, sent = [], []
    arrived = {d: [] for d in range(chips)}
    for r in range(PARTS):
        kept, given, *sent = product(r, mixed[r], other[r], pieces, own, sent)
        own = [kept, given]
        for d in EARLY:
            arrived[d].append(mirrored(sent[d], d))
    arrived[0].append(sent[0])
    for d in LATE:
        arrived[d].append(mirrored(sent[d], d))
    returned = core_swap(own[1])
    block_row = lax.dynamic_index_in_dim(blocks, perm_index, 1, keepdims=False).T
    energy_row = lax.dynamic_slice_in_dim(virtual_energy, perm_index * rows, rows, 0)[:, None]
    update = None
    for group in FINISH:
        back = jnp.array(group, jnp.int32)
        sources = (perm_index // 2 + jnp.where(perm_index % 2 == 0, chips - back, back)) % chips
        ready = [arrived[d] for d in group]
        update = finish(
            sources.astype(jnp.int32),
            tile_sizes,
            pair_energy,
            block_row,
            energy_row,
            virtual_energy.reshape(tiles, 1, TILE),
            own[0],
            returned,
            ready,
            update,
        )
    return update


def solution(mesh):
    in_specs = (
        P("wide", "perm", None),
        P("perm", None),
        P(),
        P("wide"),
        P(),
        P(),
        P("wide", None, None),
    )
    out_specs = P("wide", "perm", None)

    return jax.shard_map(
        per_device, mesh=mesh, in_specs=in_specs, out_specs=out_specs, check_vma=False
    )
```

profile of v0, /device:TPU:6, one launch (start us, length us, event | category | flops | bytes accessed | tf_op | source)
XLA Modules:
  0.0 189.6 jit_solution(3515951560062021098)
XLA Ops:
  0.0 5.3 %collective-permute-start.1 = (bf16[4,128,2048]{2,1,0:T(8,128)(2,1)}, bf16[4,128,2048]{2,1,0:T(8,128)(2,1)S(1)}, u32[]{:S(2)}, u32[]{:S(2)}) collective-permute-start(bf16[4,128,2048]{2,1,0:T(8,128)(2,1)} %own_ref.3), channel_id=1, source_target_pairs={{16,0},{32,16},{48,32},{64,48},{80,64},{96,80},{112,96},{128,112},... | collective-permute-start | bytes 6291464 | tf_op jit(solution)/shard_map/ppermute | solution.py:22
  15.1 3.2 %collective-permute-done.4.refs_6_ = bf16[64,1024]{1,0:T(8,128)(2,1)S(1)} collective-permute-done((bf16[64,1024]{1,0:T(8,128)(2,1)}, bf16[64,1024]{1,0:T(8,128)(2,1)S(1)}, u32[]{:S(2)}, u32[]{:S(2)}) %collective-permute-start.4) | collective-permute-done | bytes 131104 | tf_op jit(solution)/shard_map/ppermute | solution.py:37
  21.1 3.3 %collective-permute-done.8.refs_10_ = bf16[64,1024]{1,0:T(8,128)(2,1)S(1)} collective-permute-done((bf16[64,1024]{1,0:T(8,128)(2,1)S(1)}, bf16[64,1024]{1,0:T(8,128)(2,1)S(1)}, u32[]{:S(2)}, u32[]{:S(2)}) %collective-permute-start.8) | collective-permute-done | bytes 131104 | tf_op jit(solution)/shard_map/ppermute | solution.py:37
  25.9 24.6 %collective-permute-done.1.after_ref = bf16[4,128,2048]{2,1,0:T(8,128)(2,1)S(1)} collective-permute-done((bf16[4,128,2048]{2,1,0:T(8,128)(2,1)}, bf16[4,128,2048]{2,1,0:T(8,128)(2,1)S(1)}, u32[]{:S(2)}, u32[]{:S(2)}) %collective-permute-start.1) | collective-permute-done | bytes 2097184 | tf_op jit(solution)/shard_map/ppermute | solution.py:22
  50.5 6.2 %collective-permute-done.before_ref = bf16[4,128,2048]{2,1,0:T(8,128)(2,1)} collective-permute-done((bf16[4,128,2048]{2,1,0:T(8,128)(2,1)}, bf16[4,128,2048]{2,1,0:T(8,128)(2,1)}, u32[]{:S(2)}, u32[]{:S(2)}) %collective-permute-start) | collective-permute-done | bytes 2097184 | tf_op jit(solution)/shard_map/ppermute | solution.py:22
  56.7 4.8 %mix.3 = (bf16[4,64,2048]{2,1,0:T(8,128)(2,1)}, bf16[4,64,2048]{2,1,0:T(8,128)(2,1)}) custom-call(f32[4,9]{1,0:T(4,128)} %copy.23.coef_ref, bf16[4,128,2048]{2,1,0:T(8,128)(2,1)} %collective-permute-done.before_ref, bf16[4,128,2048]{2,1,0:T(8,128)(2,1)} %own_ref.3, bf16[4,128,2048]{2,1,0:T(8,128)(2,1)} %copy-done.1), custom_call_target="tpu_custom_call" | custom-call | flops 9437184 | bytes 4194304 | tf_op jit(solution)/shard_map/mix/pallas_call | solution.py:90
  67.4 3.1 %collective-permute-start.17 = (bf16[64,1024]{1,0:T(8,128)(2,1)S(1)}, bf16[64,1024]{1,0:T(8,128)(2,1)S(1)}, u32[]{:S(2)}, u32[]{:S(2)}) collective-permute-start(bf16[64,1024]{1,0:T(8,128)(2,1)S(1)} %collective-permute-done.13.refs_15_), channel_id=1, source_target_pairs={{0,2},{1,15},{2,4},{3,1},{4,6},{5,3},{6,8},{7,5},{8,10},{9,7},{10,... | collective-permute-start | bytes 393224 | tf_op jit(solution)/shard_map/ppermute | solution.py:37
  70.6 4.7 %mix.2 = (bf16[4,64,2048]{2,1,0:T(8,128)(2,1)}, bf16[4,64,2048]{2,1,0:T(8,128)(2,1)}) custom-call(f32[4,9]{1,0:T(4,128)} %copy.23.coef_ref, bf16[4,128,2048]{2,1,0:T(8,128)(2,1)} %collective-permute-done.before_ref, bf16[4,128,2048]{2,1,0:T(8,128)(2,1)} %own_ref.3, bf16[4,128,2048]{2,1,0:T(8,128)(2,1)} %copy-done.1), custom_call_target="tpu_custom_call" | custom-call | flops 9437184 | bytes 4194304 | tf_op jit(solution)/shard_map/mix/pallas_call | solution.py:90
  78.6 3.1 %collective-permute-done.11.refs_13_ = bf16[64,1024]{1,0:T(8,128)(2,1)S(1)} collective-permute-done((bf16[64,1024]{1,0:T(8,128)(2,1)S(1)}, bf16[64,1024]{1,0:T(8,128)(2,1)S(1)}, u32[]{:S(2)}, u32[]{:S(2)}) %collective-permute-start.11) | collective-permute-done | bytes 131104 | tf_op jit(solution)/shard_map/ppermute | solution.py:37
  84.6 3.4 %collective-permute-done.21.refs_23_ = bf16[64,1024]{1,0:T(8,128)(2,1)S(1)} collective-permute-done((bf16[64,1024]{1,0:T(8,128)(2,1)S(1)}, bf16[64,1024]{1,0:T(8,128)(2,1)S(1)}, u32[]{:S(2)}, u32[]{:S(2)}) %collective-permute-start.21) | collective-permute-done | bytes 131104 | tf_op jit(solution)/shard_map/ppermute | solution.py:37
  90.7 3.4 %collective-permute-done.24.refs_26_ = bf16[64,1024]{1,0:T(8,128)(2,1)S(1)} collective-permute-done((bf16[64,1024]{1,0:T(8,128)(2,1)S(1)}, bf16[64,1024]{1,0:T(8,128)(2,1)S(1)}, u32[]{:S(2)}, u32[]{:S(2)}) %collective-permute-start.24) | collective-permute-done | bytes 131104 | tf_op jit(solution)/shard_map/ppermute | solution.py:37
  96.9 3.4 %collective-permute-done.25.refs_27_ = bf16[64,1024]{1,0:T(8,128)(2,1)S(1)} collective-permute-done((bf16[64,1024]{1,0:T(8,128)(2,1)S(1)}, bf16[64,1024]{1,0:T(8,128)(2,1)S(1)}, u32[]{:S(2)}, u32[]{:S(2)}) %collective-permute-start.25) | collective-permute-done | bytes 131104 | tf_op jit(solution)/shard_map/ppermute | solution.py:37
  103.1 3.4 %collective-permute-done.28.refs_30_ = bf16[64,1024]{1,0:T(8,128)(2,1)S(1)} collective-permute-done((bf16[64,1024]{1,0:T(8,128)(2,1)S(1)}, bf16[64,1024]{1,0:T(8,128)(2,1)S(1)}, u32[]{:S(2)}, u32[]{:S(2)}) %collective-permute-start.28) | collective-permute-done | bytes 131104 | tf_op jit(solution)/shard_map/ppermute | solution.py:37
  109.3 3.4 %collective-permute-done.29.refs_31_ = bf16[64,1024]{1,0:T(8,128)(2,1)S(1)} collective-permute-done((bf16[64,1024]{1,0:T(8,128)(2,1)S(1)}, bf16[64,1024]{1,0:T(8,128)(2,1)S(1)}, u32[]{:S(2)}, u32[]{:S(2)}) %collective-permute-start.29) | collective-permute-done | bytes 131104 | tf_op jit(solution)/shard_map/ppermute | solution.py:37
  116.3 7.3 %product.2 = (bf16[4,128,1024]{2,1,0:T(8,128)(2,1)}, bf16[4,128,1024]{2,1,0:T(8,128)(2,1)}, bf16[2,2,2,128,128]{4,3,2,1,0:T(8,128)(2,1)}, bf16[2,2,2,128,128]{4,...) custom-call(bf16[4,64,2048]{2,1,0:T(8,128)(2,1)} %get-tuple-element., ...), custom_call_target="tpu_custom_call" | custom-call | flops 2147483648 | bytes 7340032 | tf_op jit(solution)/shard_map/product/pallas_call | solution.py:179
  124.6 7.4 %product.3 = (bf16[4,128,1024]{2,1,0:T(8,128)(2,1)}, bf16[4,128,1024]{2,1,0:T(8,128)(2,1)}, bf16[2,2,2,128,128]{4,3,2,1,0:T(8,128)(2,1)}, bf16[2,2,2,128,128]{4,...) custom-call(bf16[4,64,2048]{2,1,0:T(8,128)(2,1)} %get-tuple-element., ...), custom_call_target="tpu_custom_call", output_to_operand_aliasing={{0}: (34, {}), {1}: (35, {}), {2}: (36, {}), {3}: (37, {}),... | custom-call | flops 2147483648 | bytes 7340032 | tf_op jit(solution)/shard_map/product/pallas_call | solution.py:179
  137.5 4.5 %collective-permute-start.38 = (bf16[1,2,2,128,128]{4,3,2,1,0:T(8,128)(2,1)S(1)}, bf16[1,2,2,128,128]{4,3,2,1,0:T(8,128)(2,1)S(1)}, u32[]{:S(2)}, u32[]{:S(2)}) collective-permute-start(bf16[1,2,2,128,128]{4,3,2,1,0:T(8,128)(2,1)S(1)} %copy-done.48), channel_id=1, source_target_pairs={{0,8},{1,9},{2,10},{3,11},{4,12},{5,13},{6,14},{7,15},{8,0},{9,1},... | collective-permute-start | bytes 393224 | tf_op jit(solution)/shard_map/ppermute | solution.py:37
  142.0 4.5 %collective-permute-done.39.refs_2_ = bf16[1,2,2,128,128]{4,3,2,1,0:T(8,128)(2,1)S(1)} collective-permute-done((bf16[1,2,2,128,128]{4,3,2,1,0:T(8,128)(2,1)}, bf16[1,2,2,128,128]{4,3,2,1,0:T(8,128)(2,1)S(1)}, u32[]{:S(2)}, u32[]{:S(2)}) %collective-permute-start.39) | collective-permute-done | bytes 131104 | tf_op jit(solution)/shard_map/ppermute | solution.py:37
  148.0 5.0 %collective-permute-done.41.refs_4_ = bf16[1,2,2,128,128]{4,3,2,1,0:T(8,128)(2,1)S(1)} collective-permute-done((bf16[1,2,2,128,128]{4,3,2,1,0:T(8,128)(2,1)}, bf16[1,2,2,128,128]{4,3,2,1,0:T(8,128)(2,1)S(1)}, u32[]{:S(2)}, u32[]{:S(2)}) %collective-permute-start.41) | collective-permute-done | bytes 131104 | tf_op jit(solution)/shard_map/ppermute | solution.py:37
  153.0 9.4 %collective-permute-done.38.refs_1_ = bf16[1,2,2,128,128]{4,3,2,1,0:T(8,128)(2,1)S(1)} collective-permute-done((bf16[1,2,2,128,128]{4,3,2,1,0:T(8,128)(2,1)S(1)}, bf16[1,2,2,128,128]{4,3,2,1,0:T(8,128)(2,1)S(1)}, u32[]{:S(2)}, u32[]{:S(2)}) %collective-permute-start.38) | collective-permute-done | bytes 131104 | tf_op jit(solution)/shard_map/ppermute | solution.py:37
  162.4 7.4 %collective-permute-done.40.refs_3_ = bf16[1,2,2,128,128]{4,3,2,1,0:T(8,128)(2,1)S(1)} collective-permute-done((bf16[1,2,2,128,128]{4,3,2,1,0:T(8,128)(2,1)S(1)}, bf16[1,2,2,128,128]{4,3,2,1,0:T(8,128)(2,1)S(1)}, u32[]{:S(2)}, u32[]{:S(2)}) %collective-permute-start.40) | collective-permute-done | bytes 131104 | tf_op jit(solution)/shard_map/ppermute | solution.py:37
  170.0 3.0 %collective-permute-start.37 = (bf16[2,2,2,128,128]{4,3,2,1,0:T(8,128)(2,1)}, bf16[2,2,2,128,128]{4,3,2,1,0:T(8,128)(2,1)S(1)}, u32[]{:S(2)}, u32[]{:S(2)}) collective-permute-start(bf16[2,2,2,128,128]{4,3,2,1,0:T(8,128)(2,1)} %get-tuple-element.52), channel_id=1, source_target_pairs={{0,14},{1,3},{2,0},{3,5},{4,2},{5,7},{6,4},{7,9},{8,6},{9,11},{10,... | collective-permute-start | bytes 786440 | tf_op jit(solution)/shard_map/ppermute | solution.py:37
  176.8 5.9 %finish.2.refs_4_ = bf16[4,128,2048]{2,1,0:T(8,128)(2,1)} custom-call(s32[4]{0:T(128)} %get-tuple-element.61.source_ref, s32[16]{0:T(128)} %sizes_ref.3, f32[4]{0:T(128)} %pair_ref.3, s32[16,4]{1,0:T(8,128)} %bitcast.5, f32[128,1]{1,0:T(8,128)} %copy.22.row_ref, f32[16,1,128]{2,1,0:T(1,128)} %bitcast.7, bf16[4,128,1024]{2,1,0:T(8,128)(2,1)} %get-tuple-element.47.own_ref, ...), custom_call_target="tpu_custom_call" | custom-call | flops 5242880 | bytes 3145728 | tf_op jit(solution)/shard_map/finish/pallas_call | solution.py:249
  183.7 5.9 %finish.3 = bf16[4,128,2048]{2,1,0:T(8,128)(2,1)} custom-call(s32[4]{0:T(128)} %get-tuple-element.62.source_ref, s32[16]{0:T(128)} %sizes_ref.3, f32[4]{0:T(128)} %pair_ref.3, s32[16,4]{1,0:T(8,128)} %bitcast.6, f32[128,1]{1,0:T(8,128)} %copy.22.row_ref, f32[16,1,128]{2,1,0:T(1,128)} %bitcast.8, ...), custom_call_target="tpu_custom_call", output_to_operand_aliasing={{}: (12, {})} | custom-call | flops 5242880 | bytes 3145728 | tf_op jit(solution)/shard_map/finish/pallas_call | solution.py:249
  (175 shorter events, 53.7 us)
Async XLA Ops:
  0.0 50.5 %collective-permute-start.1 = (bf16[4,128,2048]{2,1,0:T(8,128)(2,1)}, bf16[4,128,2048]{2,1,0:T(8,128)(2,1)S(1)}, u32[]{:S(2)}, u32[]{:S(2)}) collective-permute-start(bf16[4,128,2048]{2,1,0:T(8,128)(2,1)} %own_ref.3), channel_id=1, source_target_pairs={{16,0},{32,16},{48,32},{64,48},{80,64},{96,80},{112,96},{128,112},... | collective-permute-start | bytes 6291464 | tf_op jit(solution)/shard_map/ppermute | solution.py:22
  5.3 51.4 %collective-permute-start = (bf16[4,128,2048]{2,1,0:T(8,128)(2,1)}, bf16[4,128,2048]{2,1,0:T(8,128)(2,1)}, u32[]{:S(2)}, u32[]{:S(2)}) collective-permute-start(bf16[4,128,2048]{2,1,0:T(8,128)(2,1)} %own_ref.3), channel_id=1, source_target_pairs={{0,16},{16,32},{32,48},{48,64},{64,80},{80,96},{96,112},{112,128},... | collective-permute-start | bytes 6291464 | tf_op jit(solution)/shard_map/ppermute | solution.py:22
  9.2 9.0 %collective-permute-start.4 = (bf16[64,1024]{1,0:T(8,128)(2,1)}, bf16[64,1024]{1,0:T(8,128)(2,1)S(1)}, u32[]{:S(2)}, u32[]{:S(2)}) collective-permute-start(bf16[64,1024]{1,0:T(8,128)(2,1)} %get-tuple-element.34.refs_2_), channel_id=1, source_target_pairs={{0,2},{1,15},{2,4},{3,1},{4,6},{5,3},{6,8},{7,5},{8,10},{9,7},{10,... | collective-permute-start | bytes 393224 | tf_op jit(solution)/shard_map/ppermute | solution.py:37
  11.1 8.5 %collective-permute-start.5 = (bf16[64,1024]{1,0:T(8,128)(2,1)}, bf16[64,1024]{1,0:T(8,128)(2,1)S(1)}, u32[]{:S(2)}, u32[]{:S(2)}) collective-permute-start(bf16[64,1024]{1,0:T(8,128)(2,1)} %get-tuple-element.35.refs_3_), channel_id=1, source_target_pairs={{0,2},{1,15},{2,4},{3,1},{4,6},{5,3},{6,8},{7,5},{8,10},{9,7},{10,... | collective-permute-start | bytes 393224 | tf_op jit(solution)/shard_map/ppermute | solution.py:37
  13.1 48.5 %collective-permute-start.3 = (bf16[128,1024]{1,0:T(8,128)(2,1)}, bf16[128,1024]{1,0:T(8,128)(2,1)S(1)}, u32[]{:S(2)}, u32[]{:S(2)}) collective-permute-start(bf16[128,1024]{1,0:T(8,128)(2,1)} %get-tuple-element.36), channel_id=1, source_target_pairs={{0,1},{1,0},{2,3},{3,2},{4,5},{5,4},{6,7},{7,6},{8,9},{9,8},{10,11... | collective-permute-start | bytes 786440 | tf_op jit(solution)/shard_map/ppermute | solution.py:27
  24.4 41.1 %collective-permute-start.12 = (bf16[64,1024]{1,0:T(8,128)(2,1)S(1)}, bf16[64,1024]{1,0:T(8,128)(2,1)S(1)}, u32[]{:S(2)}, u32[]{:S(2)}) collective-permute-start(bf16[64,1024]{1,0:T(8,128)(2,1)S(1)} %collective-permute-done.8.refs_10_), channel_id=1, source_target_pairs={{0,2},{1,15},{2,4},{3,1},{4,6},{5,3},{6,8},{7,5},{8,10},{9,7},{10,... | collective-permute-start | bytes 393224 | tf_op jit(solution)/shard_map/ppermute | solution.py:37
  25.8 41.6 %collective-permute-start.13 = (bf16[64,1024]{1,0:T(8,128)(2,1)S(1)}, bf16[64,1024]{1,0:T(8,128)(2,1)S(1)}, u32[]{:S(2)}, u32[]{:S(2)}) collective-permute-start(bf16[64,1024]{1,0:T(8,128)(2,1)S(1)} %collective-permute-done.9.refs_11_), channel_id=1, source_target_pairs={{0,2},{1,15},{2,4},{3,1},{4,6},{5,3},{6,8},{7,5},{8,10},{9,7},{10,... | collective-permute-start | bytes 393224 | tf_op jit(solution)/shard_map/ppermute | solution.py:37
  61.5 53.9 %collective-permute-start.32 = (bf16[4,64,2048]{2,1,0:T(8,128)(2,1)}, bf16[4,64,2048]{2,1,0:T(8,128)(2,1)}, u32[]{:S(2)}, u32[]{:S(2)}) collective-permute-start(bf16[4,64,2048]{2,1,0:T(8,128)(2,1)} %get-tuple-element.38), channel_id=1, source_target_pairs={{0,1},{1,0},{2,3},{3,2},{4,5},{5,4},{6,7},{7,6},{8,9},{9,8},{10,11... | collective-permute-start | bytes 3145736 | tf_op jit(solution)/shard_map/ppermute | solution.py:27
  61.6 13.8 %collective-permute-start.7 = (bf16[64,1024]{1,0:T(8,128)(2,1)S(1)}, bf16[64,1024]{1,0:T(8,128)(2,1)S(1)}, u32[]{:S(2)}, u32[]{:S(2)}) collective-permute-start(bf16[64,1024]{1,0:T(8,128)(2,1)S(1)} %get-tuple-element.59.refs_5_), channel_id=1, source_target_pairs={{0,2},{1,15},{2,4},{3,1},{4,6},{5,3},{6,8},{7,5},{8,10},{9,7},{10,... | collective-permute-start | bytes 393224 | tf_op jit(solution)/shard_map/ppermute | solution.py:37
  63.6 11.9 %collective-permute-start.6 = (bf16[64,1024]{1,0:T(8,128)(2,1)S(1)}, bf16[64,1024]{1,0:T(8,128)(2,1)S(1)}, u32[]{:S(2)}, u32[]{:S(2)}) collective-permute-start(bf16[64,1024]{1,0:T(8,128)(2,1)S(1)} %get-tuple-element.60.refs_4_), channel_id=1, source_target_pairs={{0,2},{1,15},{2,4},{3,1},{4,6},{5,3},{6,8},{7,5},{8,10},{9,7},{10,... | collective-permute-start | bytes 393224 | tf_op jit(solution)/shard_map/ppermute | solution.py:37
  65.5 11.1 %collective-permute-start.16 = (bf16[64,1024]{1,0:T(8,128)(2,1)S(1)}, bf16[64,1024]{1,0:T(8,128)(2,1)S(1)}, u32[]{:S(2)}, u32[]{:S(2)}) collective-permute-start(bf16[64,1024]{1,0:T(8,128)(2,1)S(1)} %collective-permute-done.12.refs_14_), channel_id=1, source_target_pairs={{0,2},{1,15},{2,4},{3,1},{4,6},{5,3},{6,8},{7,5},{8,10},{9,7},{10,... | collective-permute-start | bytes 393224 | tf_op jit(solution)/shard_map/ppermute | solution.py:37
  67.4 10.2 %collective-permute-start.17 = (bf16[64,1024]{1,0:T(8,128)(2,1)S(1)}, bf16[64,1024]{1,0:T(8,128)(2,1)S(1)}, u32[]{:S(2)}, u32[]{:S(2)}) collective-permute-start(bf16[64,1024]{1,0:T(8,128)(2,1)S(1)} %collective-permute-done.13.refs_15_), channel_id=1, source_target_pairs={{0,2},{1,15},{2,4},{3,1},{4,6},{5,3},{6,8},{7,5},{8,10},{9,7},{10,... | collective-permute-start | bytes 393224 | tf_op jit(solution)/shard_map/ppermute | solution.py:37
  75.4 48.2 %collective-permute-start.2 = (bf16[4,64,2048]{2,1,0:T(8,128)(2,1)}, bf16[4,64,2048]{2,1,0:T(8,128)(2,1)S(1)}, u32[]{:S(2)}, u32[]{:S(2)}) collective-permute-start(bf16[4,64,2048]{2,1,0:T(8,128)(2,1)} %get-tuple-element.33), channel_id=1, source_target_pairs={{0,1},{1,0},{2,3},{3,2},{4,5},{5,4},{6,7},{7,6},{8,9},{9,8},{10,11... | collective-permute-start | bytes 3145736 | tf_op jit(solution)/shard_map/ppermute | solution.py:27
  77.6 6.9 %collective-permute-start.20 = (bf16[64,1024]{1,0:T(8,128)(2,1)S(1)}, bf16[64,1024]{1,0:T(8,128)(2,1)S(1)}, u32[]{:S(2)}, u32[]{:S(2)}) collective-permute-start(bf16[64,1024]{1,0:T(8,128)(2,1)S(1)} %collective-permute-done.16.refs_18_), channel_id=1, source_target_pairs={{0,2},{1,15},{2,4},{3,1},{4,6},{5,3},{6,8},{7,5},{8,10},{9,7},{10,... | collective-permute-start | bytes 393224 | tf_op jit(solution)/shard_map/ppermute | solution.py:37
  132.0 43.8 %collective-permute-start.33 = (bf16[4,128,1024]{2,1,0:T(8,128)(2,1)}, bf16[4,128,1024]{2,1,0:T(8,128)(2,1)S(1)}, u32[]{:S(2)}, u32[]{:S(2)}) collective-permute-start(bf16[4,128,1024]{2,1,0:T(8,128)(2,1)} %get-tuple-element.48), channel_id=1, source_target_pairs={{0,1},{1,0},{2,3},{3,2},{4,5},{5,4},{6,7},{7,6},{8,9},{9,8},{10,11... | collective-permute-start | bytes 3145736 | tf_op jit(solution)/shard_map/ppermute | solution.py:27
  132.1 14.4 %collective-permute-start.39 = (bf16[1,2,2,128,128]{4,3,2,1,0:T(8,128)(2,1)}, bf16[1,2,2,128,128]{4,3,2,1,0:T(8,128)(2,1)S(1)}, u32[]{:S(2)}, u32[]{:S(2)}) collective-permute-start(bf16[1,2,2,128,128]{4,3,2,1,0:T(8,128)(2,1)} %get-tuple-element.55), channel_id=1, source_target_pairs={{0,8},{1,9},{2,10},{3,11},{4,12},{5,13},{6,14},{7,15},{8,0},{9,1},... | collective-permute-start | bytes 393224 | tf_op jit(solution)/shard_map/ppermute | solution.py:37
  133.7 36.4 %collective-permute-start.42 = (bf16[2,2,2,128,128]{4,3,2,1,0:T(8,128)(2,1)}, bf16[2,2,2,128,128]{4,3,2,1,0:T(8,128)(2,1)S(1)}, u32[]{:S(2)}, u32[]{:S(2)}) collective-permute-start(bf16[2,2,2,128,128]{4,3,2,1,0:T(8,128)(2,1)} %get-tuple-element.58), channel_id=1, source_target_pairs={{0,10},{1,7},{2,12},{3,9},{4,14},{5,11},{6,0},{7,13},{8,2},{9,15},... | collective-permute-start | bytes 786440 | tf_op jit(solution)/shard_map/ppermute | solution.py:37
  135.5 17.5 %collective-permute-start.41 = (bf16[1,2,2,128,128]{4,3,2,1,0:T(8,128)(2,1)}, bf16[1,2,2,128,128]{4,3,2,1,0:T(8,128)(2,1)S(1)}, u32[]{:S(2)}, u32[]{:S(2)}) collective-permute-start(bf16[1,2,2,128,128]{4,3,2,1,0:T(8,128)(2,1)} %get-tuple-element.57), channel_id=1, source_target_pairs={{0,6},{1,11},{2,8},{3,13},{4,10},{5,15},{6,12},{7,1},{8,14},{9,3},... | collective-permute-start | bytes 393224 | tf_op jit(solution)/shard_map/ppermute | solution.py:37
  137.5 24.9 %collective-permute-start.38 = (bf16[1,2,2,128,128]{4,3,2,1,0:T(8,128)(2,1)S(1)}, bf16[1,2,2,128,128]{4,3,2,1,0:T(8,128)(2,1)S(1)}, u32[]{:S(2)}, u32[]{:S(2)}) collective-permute-start(bf16[1,2,2,128,128]{4,3,2,1,0:T(8,128)(2,1)S(1)} %copy-done.48), channel_id=1, source_target_pairs={{0,8},{1,9},{2,10},{3,11},{4,12},{5,13},{6,14},{7,15},{8,0},{9,1},... | collective-permute-start | bytes 393224 | tf_op jit(solution)/shard_map/ppermute | solution.py:37
  146.5 23.3 %collective-permute-start.40 = (bf16[1,2,2,128,128]{4,3,2,1,0:T(8,128)(2,1)S(1)}, bf16[1,2,2,128,128]{4,3,2,1,0:T(8,128)(2,1)S(1)}, u32[]{:S(2)}, u32[]{:S(2)}) collective-permute-start(bf16[1,2,2,128,128]{4,3,2,1,0:T(8,128)(2,1)S(1)} %copy-done.47), channel_id=1, source_target_pairs={{0,6},{1,11},{2,8},{3,13},{4,10},{5,15},{6,12},{7,1},{8,14},{9,3},... | collective-permute-start | bytes 393224 | tf_op jit(solution)/shard_map/ppermute | solution.py:37
  153.0 29.7 %collective-permute-start.34 = (bf16[2,2,2,128,128]{4,3,2,1,0:T(8,128)(2,1)}, bf16[2,2,2,128,128]{4,3,2,1,0:T(8,128)(2,1)S(1)}, u32[]{:S(2)}, u32[]{:S(2)}) collective-permute-start(bf16[2,2,2,128,128]{4,3,2,1,0:T(8,128)(2,1)} %get-tuple-element.49), channel_id=1, source_target_pairs={{0,4},{1,13},{2,6},{3,15},{4,8},{5,1},{6,10},{7,3},{8,12},{9,5},{1... | collective-permute-start | bytes 786440 | tf_op jit(solution)/shard_map/ppermute | solution.py:37
  162.4 20.3 %collective-permute-start.35 = (bf16[2,2,2,128,128]{4,3,2,1,0:T(8,128)(2,1)}, bf16[2,2,2,128,128]{4,3,2,1,0:T(8,128)(2,1)S(1)}, u32[]{:S(2)}, u32[]{:S(2)}) collective-permute-start(bf16[2,2,2,128,128]{4,3,2,1,0:T(8,128)(2,1)} %get-tuple-element.50), channel_id=1, source_target_pairs={{0,12},{1,5},{2,14},{3,7},{4,0},{5,9},{6,2},{7,11},{8,4},{9,13},{1... | collective-permute-start | bytes 786440 | tf_op jit(solution)/shard_map/ppermute | solution.py:37
  169.8 12.9 %collective-permute-start.36 = (bf16[2,2,2,128,128]{4,3,2,1,0:T(8,128)(2,1)}, bf16[2,2,2,128,128]{4,3,2,1,0:T(8,128)(2,1)S(1)}, u32[]{:S(2)}, u32[]{:S(2)}) collective-permute-start(bf16[2,2,2,128,128]{4,3,2,1,0:T(8,128)(2,1)} %get-tuple-element.51), channel_id=1, source_target_pairs={{0,2},{1,15},{2,4},{3,1},{4,6},{5,3},{6,8},{7,5},{8,10},{9,7},{10,... | collective-permute-start | bytes 786440 | tf_op jit(solution)/shard_map/ppermute | solution.py:37
  170.0 12.7 %collective-permute-start.37 = (bf16[2,2,2,128,128]{4,3,2,1,0:T(8,128)(2,1)}, bf16[2,2,2,128,128]{4,3,2,1,0:T(8,128)(2,1)S(1)}, u32[]{:S(2)}, u32[]{:S(2)}) collective-permute-start(bf16[2,2,2,128,128]{4,3,2,1,0:T(8,128)(2,1)} %get-tuple-element.52), channel_id=1, source_target_pairs={{0,14},{1,3},{2,0},{3,5},{4,2},{5,7},{6,4},{7,9},{8,6},{9,11},{10,... | collective-permute-start | bytes 786440 | tf_op jit(solution)/shard_map/ppermute | solution.py:37
  (68 other events, 1322.9 us)
where the time goes:
time: 191 us; the launch traced here: 190 us
  waiting for transfers between devices  103 us (54%)
  starting transfers between devices  40.2 us (21%)
  Pallas kernels  38 us (20%)
  local copies, waits for them, and re-layouts  7.28 us (4%)
    ppermute x37, waiting for transfers between devices, mirrored(): return lax.ppermute(block, 'perm', route)  72.3 us
    ppermute x2, waiting for transfers between devices, wide_shift(): return lax.ppermute(block, 'wide', route)  30.8 us
    ppermute x37, starting transfers between devices, mirrored(): return lax.ppermute(block, 'perm', route)  30.7 us
    pallas_call x2, Pallas kernels, product(): pl.pallas_call(functools.partial(product_body, len(pieces), chips), out_s...  14.7 us
    pallas_call x2, Pallas kernels, finish(): pl.pallas_call(functools.partial(finish_body, splits), out_shape=jax.Shap...  11.8 us
    pallas_call x2, Pallas kernels, mix(): pl.pallas_call(mix_body, out_shape=[jax.ShapeDtypeStruct((pairs, rows, wi...  9.52 us
    ppermute x2, starting transfers between devices, wide_shift(): return lax.ppermute(block, 'wide', route)  7.23 us
    unnamed x99, local copies, waits for them, and re-layouts  4.32 us
  transfers between devices with their start and end apart: 43, of which 28 were waited for; matrix products, arithmetic and copies ran while one was open for 2% of the time, Pallas kernels for 13%

commit v1 on v0

--- a/solution.py
+++ b/solution.py
@@ -9,6 +9,7 @@
 
 
 TILE = 128
+ALL_VMEM = pltpu.CompilerParams(vmem_limit_bytes=67_043_328)
 PARTS = 2
 STREAMS = 4
 EARLY = (3, 4)
@@ -51,7 +52,8 @@
 
 def mix_body(coef_ref, before_ref, own_ref, after_ref, *mixed_refs):
     pairs, rows, width = own_ref.shape
-    taps = coef_ref.shape[1]
+    taps = coef_ref.shape[0]
+    first = lax.axis_index("wide") * pairs
     chips = width // TILE // 2
     step = 32
 
@@ -69,7 +71,7 @@
                 value = ref[q % pairs, start : start + step, source].astype(jnp.float32)
                 for p in range(pairs):
                     if 0 <= q - p < taps:
-                        term = coef_ref[p, q - p] * value
+                        term = coef_ref[q - p, first + p] * value
                         total[p] = term if total[p] is None else total[p] + term
             for p in range(pairs):
                 rounded = total[p].astype(jnp.bfloat16)
@@ -96,6 +98,7 @@
         cost_estimate=pl.CostEstimate(
             flops=18 * pairs * rows * width, bytes_accessed=8 * pairs * rows * width, transcendentals=0
         ),
+        compiler_params=ALL_VMEM,
         name="mix",
     )(coef, before, own, after)
 
@@ -190,6 +193,7 @@
             bytes_accessed=4 * pairs * rows * (width + columns) + 2 * width * columns,
             transcendentals=0,
         ),
+        compiler_params=ALL_VMEM,
         name="product",
     )(mixed, other, *pieces, *targets)
 
@@ -271,6 +275,7 @@
             bytes_accessed=12 * count * pairs * rows * TILE,
             transcendentals=0,
         ),
+        compiler_params=ALL_VMEM,
         name="finish",
     )(
         sources,
@@ -287,12 +292,11 @@
 
 
 def per_device(amplitudes, integrals, coupling, pair_energy, virtual_energy, tile_sizes, blocks):
-    pairs, rows, _ = amplitudes.shape
+    _, rows, _ = amplitudes.shape
     tiles = tile_sizes.shape[0]
     chips = tiles // 2
-    wide_index = lax.axis_index("wide")
     perm_index = lax.axis_index("perm")
-    coef = lax.dynamic_slice_in_dim(coupling, wide_index * pairs, pairs, 0)
+    coef = coupling.T
     before = wide_shift(amplitudes, 1)
     after = wide_shift(amplitudes, -1)
     *kept_columns, given_columns = split(integrals)

time: 191 us -> 191 us (level)
  waiting for transfers between devices: 103 us -> 105 us
    unnamed x99 -> x40, local copies, waits for them, and re-layouts: 4.32 us -> 1.31 us
    ppermute x37, waiting for transfers between devices: 72.3 us -> 74.7 us  [mirrored(): return lax.ppermute(block, 'perm', route)]
  transfers between devices with their start and end apart: 43 -> 43, of which waited for: 28 -> 28; matrix products, arithmetic and copies ran while one was open for 2% -> 3% of each run, Pallas kernels for 13% -> 13%
where the time goes in v1:
time: 191 us; the launch traced here: 190 us
  waiting for transfers between devices  105 us (55%)
  starting transfers between devices  39.8 us (21%)
  Pallas kernels  38.1 us (20%)
  local copies, waits for them, and re-layouts  5.87 us (3%)
    ppermute x37, waiting for transfers between devices, mirrored(): return lax.ppermute(block, 'perm', route)  74.7 us
    ppermute x37, starting transfers between devices, mirrored(): return lax.ppermute(block, 'perm', route)  30.5 us
    ppermute x2, waiting for transfers between devices, wide_shift(): return lax.ppermute(block, 'wide', route)  30.2 us
    pallas_call x2, Pallas kernels, product(): pl.pallas_call(functools.partial(product_body, len(pieces), chips), out_s...  14.5 us
    pallas_call x2, Pallas kernels, finish(): pl.pallas_call(functools.partial(finish_body, splits), out_shape=jax.Shap...  11.8 us
    pallas_call x2, Pallas kernels, mix(): pl.pallas_call(mix_body, out_shape=[jax.ShapeDtypeStruct((pairs, rows, wi...  9.79 us
    ppermute x2, starting transfers between devices, wide_shift(): return lax.ppermute(block, 'wide', route)  7.1 us
  transfers between devices with their start and end apart: 43, of which 28 were waited for; matrix products, arithmetic and copies ran while one was open for 3% of the time, Pallas kernels for 13%

profile of v1, /device:TPU:6, one launch (start us, length us, event | category | flops | bytes accessed | tf_op | source)
XLA Modules:
  0.0 190.1 jit_solution(3033927474441062552)
XLA Ops:
  0.0 5.2 %collective-permute-start.1 = (bf16[4,128,2048]{2,1,0:T(8,128)(2,1)}, bf16[4,128,2048]{2,1,0:T(8,128)(2,1)}, u32[]{:S(2)}, u32[]{:S(2)}) collective-permute-start(bf16[4,128,2048]{2,1,0:T(8,128)(2,1)} %own_ref.3), channel_id=1, source_target_pairs={{16,0},{32,16},{48,32},{64,48},{80,64},{96,80},{112,96},{128,112},... | collective-permute-start | bytes 6291464 | tf_op jit(solution)/shard_map/ppermute | solution.py:23
  14.9 3.2 %collective-permute-done.4.refs_6_ = bf16[64,1024]{1,0:T(8,128)(2,1)S(1)} collective-permute-done((bf16[64,1024]{1,0:T(8,128)(2,1)}, bf16[64,1024]{1,0:T(8,128)(2,1)S(1)}, u32[]{:S(2)}, u32[]{:S(2)}) %collective-permute-start.4) | collective-permute-done | bytes 131104 | tf_op jit(solution)/shard_map/ppermute | solution.py:38
  19.5 5.5 %collective-permute-done.8.refs_10_ = bf16[64,1024]{1,0:T(8,128)(2,1)} collective-permute-done((bf16[64,1024]{1,0:T(8,128)(2,1)S(1)}, bf16[64,1024]{1,0:T(8,128)(2,1)}, u32[]{:S(2)}, u32[]{:S(2)}) %collective-permute-start.8) | collective-permute-done | bytes 131104 | tf_op jit(solution)/shard_map/ppermute | solution.py:38
  26.4 23.9 %collective-permute-done.1.after_ref = bf16[4,128,2048]{2,1,0:T(8,128)(2,1)} collective-permute-done((bf16[4,128,2048]{2,1,0:T(8,128)(2,1)}, bf16[4,128,2048]{2,1,0:T(8,128)(2,1)}, u32[]{:S(2)}, u32[]{:S(2)}) %collective-permute-start.1) | collective-permute-done | bytes 2097184 | tf_op jit(solution)/shard_map/ppermute | solution.py:23
  50.4 6.2 %collective-permute-done.before_ref = bf16[4,128,2048]{2,1,0:T(8,128)(2,1)} collective-permute-done((bf16[4,128,2048]{2,1,0:T(8,128)(2,1)}, bf16[4,128,2048]{2,1,0:T(8,128)(2,1)}, u32[]{:S(2)}, u32[]{:S(2)}) %collective-permute-start) | collective-permute-done | bytes 2097184 | tf_op jit(solution)/shard_map/ppermute | solution.py:23
  56.6 4.9 %mix.3 = (bf16[4,64,2048]{2,1,0:T(8,128)(2,1)}, bf16[4,64,2048]{2,1,0:T(8,128)(2,1)}) custom-call(f32[9,64]{1,0:T(8,128)} %bitcast.8, bf16[4,128,2048]{2,1,0:T(8,128)(2,1)} %collective-permute-done.before_ref, bf16[4,128,2048]{2,1,0:T(8,128)(2,1)} %own_ref.3, bf16[4,128,2048]{2,1,0:T(8,128)(2,1)} %collective-permute-done.1.after_ref), custom_call_target="tpu_custom_call" | custom-call | flops 9437184 | bytes 4194304 | tf_op jit(solution)/shard_map/mix/pallas_call | solution.py:92
  68.9 3.1 %collective-permute-start.17 = (bf16[64,1024]{1,0:T(8,128)(2,1)}, bf16[64,1024]{1,0:T(8,128)(2,1)}, u32[]{:S(2)}, u32[]{:S(2)}) collective-permute-start(bf16[64,1024]{1,0:T(8,128)(2,1)} %collective-permute-done.13.refs_15_), channel_id=1, source_target_pairs={{0,2},{1,15},{2,4},{3,1},{4,6},{5,3},{6,8},{7,5},{8,10},{9,7},{10,... | collective-permute-start | bytes 393224 | tf_op jit(solution)/shard_map/ppermute | solution.py:38
  72.1 4.9 %mix.2 = (bf16[4,64,2048]{2,1,0:T(8,128)(2,1)}, bf16[4,64,2048]{2,1,0:T(8,128)(2,1)}) custom-call(f32[9,64]{1,0:T(8,128)} %bitcast.9, bf16[4,128,2048]{2,1,0:T(8,128)(2,1)} %collective-permute-done.before_ref, bf16[4,128,2048]{2,1,0:T(8,128)(2,1)} %own_ref.3, bf16[4,128,2048]{2,1,0:T(8,128)(2,1)} %collective-permute-done.1.after_ref), custom_call_target="tpu_custom_call" | custom-call | flops 9437184 | bytes 4194304 | tf_op jit(solution)/shard_map/mix/pallas_call | solution.py:92
  80.2 3.3 %collective-permute-done.11.refs_13_ = bf16[64,1024]{1,0:T(8,128)(2,1)S(1)} collective-permute-done((bf16[64,1024]{1,0:T(8,128)(2,1)}, bf16[64,1024]{1,0:T(8,128)(2,1)S(1)}, u32[]{:S(2)}, u32[]{:S(2)}) %collective-permute-start.11) | collective-permute-done | bytes 131104 | tf_op jit(solution)/shard_map/ppermute | solution.py:38
  86.3 3.6 %collective-permute-done.21.refs_23_ = bf16[64,1024]{1,0:T(8,128)(2,1)S(1)} collective-permute-done((bf16[64,1024]{1,0:T(8,128)(2,1)}, bf16[64,1024]{1,0:T(8,128)(2,1)S(1)}, u32[]{:S(2)}, u32[]{:S(2)}) %collective-permute-start.21) | collective-permute-done | bytes 131104 | tf_op jit(solution)/shard_map/ppermute | solution.py:38
  92.7 3.4 %collective-permute-done.24.refs_26_ = bf16[64,1024]{1,0:T(8,128)(2,1)S(1)} collective-permute-done((bf16[64,1024]{1,0:T(8,128)(2,1)S(1)}, bf16[64,1024]{1,0:T(8,128)(2,1)S(1)}, u32[]{:S(2)}, u32[]{:S(2)}) %collective-permute-start.24) | collective-permute-done | bytes 131104 | tf_op jit(solution)/shard_map/ppermute | solution.py:38
  98.9 3.4 %collective-permute-done.25.refs_27_ = bf16[64,1024]{1,0:T(8,128)(2,1)S(1)} collective-permute-done((bf16[64,1024]{1,0:T(8,128)(2,1)S(1)}, bf16[64,1024]{1,0:T(8,128)(2,1)S(1)}, u32[]{:S(2)}, u32[]{:S(2)}) %collective-permute-start.25) | collective-permute-done | bytes 131104 | tf_op jit(solution)/shard_map/ppermute | solution.py:38
  105.1 3.4 %collective-permute-done.28.refs_30_ = bf16[64,1024]{1,0:T(8,128)(2,1)S(1)} collective-permute-done((bf16[64,1024]{1,0:T(8,128)(2,1)S(1)}, bf16[64,1024]{1,0:T(8,128)(2,1)S(1)}, u32[]{:S(2)}, u32[]{:S(2)}) %collective-permute-start.28) | collective-permute-done | bytes 131104 | tf_op jit(solution)/shard_map/ppermute | solution.py:38
  111.2 3.4 %collective-permute-done.29.refs_31_ = bf16[64,1024]{1,0:T(8,128)(2,1)S(1)} collective-permute-done((bf16[64,1024]{1,0:T(8,128)(2,1)S(1)}, bf16[64,1024]{1,0:T(8,128)(2,1)S(1)}, u32[]{:S(2)}, u32[]{:S(2)}) %collective-permute-start.29) | collective-permute-done | bytes 131104 | tf_op jit(solution)/shard_map/ppermute | solution.py:38
  118.1 7.3 %product.2 = (bf16[4,128,1024]{2,1,0:T(8,128)(2,1)}, bf16[4,128,1024]{2,1,0:T(8,128)(2,1)}, bf16[2,2,2,128,128]{4,3,2,1,0:T(8,128)(2,1)}, bf16[2,2,2,128,128]{4,...) custom-call(bf16[4,64,2048]{2,1,0:T(8,128)(2,1)} %get-tuple-element., ...), custom_call_target="tpu_custom_call" | custom-call | flops 2147483648 | bytes 7340032 | tf_op jit(solution)/shard_map/product/pallas_call | solution.py:182
  125.4 7.3 %product.3 = (bf16[4,128,1024]{2,1,0:T(8,128)(2,1)}, bf16[4,128,1024]{2,1,0:T(8,128)(2,1)}, bf16[2,2,2,128,128]{4,3,2,1,0:T(8,128)(2,1)}, bf16[2,2,2,128,128]{4,...) custom-call(bf16[4,64,2048]{2,1,0:T(8,128)(2,1)} %get-tuple-element., ...), custom_call_target="tpu_custom_call", output_to_operand_aliasing={{0}: (34, {}), {1}: (35, {}), {2}: (36, {}), {3}: (37, {}),... | custom-call | flops 2147483648 | bytes 7340032 | tf_op jit(solution)/shard_map/product/pallas_call | solution.py:182
  138.1 4.5 %collective-permute-start.38 = (bf16[1,2,2,128,128]{4,3,2,1,0:T(8,128)(2,1)}, bf16[1,2,2,128,128]{4,3,2,1,0:T(8,128)(2,1)}, u32[]{:S(2)}, u32[]{:S(2)}) collective-permute-start(bf16[1,2,2,128,128]{4,3,2,1,0:T(8,128)(2,1)} %get-tuple-element.54), channel_id=1, source_target_pairs={{0,8},{1,9},{2,10},{3,11},{4,12},{5,13},{6,14},{7,15},{8,0},{9,1},... | collective-permute-start | bytes 393224 | tf_op jit(solution)/shard_map/ppermute | solution.py:38
  142.6 4.7 %collective-permute-done.39.refs_2_ = bf16[1,2,2,128,128]{4,3,2,1,0:T(8,128)(2,1)} collective-permute-done((bf16[1,2,2,128,128]{4,3,2,1,0:T(8,128)(2,1)}, bf16[1,2,2,128,128]{4,3,2,1,0:T(8,128)(2,1)}, u32[]{:S(2)}, u32[]{:S(2)}) %collective-permute-start.39) | collective-permute-done | bytes 131104 | tf_op jit(solution)/shard_map/ppermute | solution.py:38
  149.5 4.4 %collective-permute-done.41.refs_4_ = bf16[1,2,2,128,128]{4,3,2,1,0:T(8,128)(2,1)} collective-permute-done((bf16[1,2,2,128,128]{4,3,2,1,0:T(8,128)(2,1)}, bf16[1,2,2,128,128]{4,3,2,1,0:T(8,128)(2,1)}, u32[]{:S(2)}, u32[]{:S(2)}) %collective-permute-start.41) | collective-permute-done | bytes 131104 | tf_op jit(solution)/shard_map/ppermute | solution.py:38
  153.9 9.4 %collective-permute-done.38.refs_1_ = bf16[1,2,2,128,128]{4,3,2,1,0:T(8,128)(2,1)} collective-permute-done((bf16[1,2,2,128,128]{4,3,2,1,0:T(8,128)(2,1)}, bf16[1,2,2,128,128]{4,3,2,1,0:T(8,128)(2,1)}, u32[]{:S(2)}, u32[]{:S(2)}) %collective-permute-start.38) | collective-permute-done | bytes 131104 | tf_op jit(solution)/shard_map/ppermute | solution.py:38
  163.3 8.3 %collective-permute-done.40.refs_3_ = bf16[1,2,2,128,128]{4,3,2,1,0:T(8,128)(2,1)} collective-permute-done((bf16[1,2,2,128,128]{4,3,2,1,0:T(8,128)(2,1)}, bf16[1,2,2,128,128]{4,3,2,1,0:T(8,128)(2,1)}, u32[]{:S(2)}, u32[]{:S(2)}) %collective-permute-start.40) | collective-permute-done | bytes 131104 | tf_op jit(solution)/shard_map/ppermute | solution.py:38
  171.6 3.2 %collective-permute-start.37 = (bf16[2,2,2,128,128]{4,3,2,1,0:T(8,128)(2,1)}, bf16[2,2,2,128,128]{4,3,2,1,0:T(8,128)(2,1)}, u32[]{:S(2)}, u32[]{:S(2)}) collective-permute-start(bf16[2,2,2,128,128]{4,3,2,1,0:T(8,128)(2,1)} %get-tuple-element.52), channel_id=1, source_target_pairs={{0,14},{1,3},{2,0},{3,5},{4,2},{5,7},{6,4},{7,9},{8,6},{9,11},{10,... | collective-permute-start | bytes 786440 | tf_op jit(solution)/shard_map/ppermute | solution.py:38
  178.3 5.9 %finish.2.refs_4_ = bf16[4,128,2048]{2,1,0:T(8,128)(2,1)} custom-call(s32[4]{0:T(128)} %get-tuple-element.61.source_ref, s32[16]{0:T(128)} %sizes_ref.3, f32[4]{0:T(128)} %pair_ref.3, s32[16,4]{1,0:T(8,128)} %bitcast.6, f32[128,1]{1,0:T(8,128)} %copy.21.row_ref, f32[16,1,128]{2,1,0:T(1,128)} %bitcast.10, bf16[4,128,1024]{2,1,0:T(8,128)(2,1)} %get-tuple-element.47.own_ref, ...), custom_call_target="tpu_custom_call" | custom-call | flops 5242880 | bytes 3145728 | tf_op jit(solution)/shard_map/finish/pallas_call | solution.py:253
  184.2 5.9 %finish.3 = bf16[4,128,2048]{2,1,0:T(8,128)(2,1)} custom-call(s32[4]{0:T(128)} %get-tuple-element.62.source_ref, s32[16]{0:T(128)} %sizes_ref.3, f32[4]{0:T(128)} %pair_ref.3, s32[16,4]{1,0:T(8,128)} %bitcast.7, f32[128,1]{1,0:T(8,128)} %copy.21.row_ref, f32[16,1,128]{2,1,0:T(1,128)} %bitcast.11, ...), custom_call_target="tpu_custom_call", output_to_operand_aliasing={{}: (12, {})} | custom-call | flops 5242880 | bytes 3145728 | tf_op jit(solution)/shard_map/finish/pallas_call | solution.py:253
  (115 shorter events, 51.8 us)
Async XLA Ops:
  0.0 50.4 %collective-permute-start.1 = (bf16[4,128,2048]{2,1,0:T(8,128)(2,1)}, bf16[4,128,2048]{2,1,0:T(8,128)(2,1)}, u32[]{:S(2)}, u32[]{:S(2)}) collective-permute-start(bf16[4,128,2048]{2,1,0:T(8,128)(2,1)} %own_ref.3), channel_id=1, source_target_pairs={{16,0},{32,16},{48,32},{64,48},{80,64},{96,80},{112,96},{128,112},... | collective-permute-start | bytes 6291464 | tf_op jit(solution)/shard_map/ppermute | solution.py:23
  5.2 51.4 %collective-permute-start = (bf16[4,128,2048]{2,1,0:T(8,128)(2,1)}, bf16[4,128,2048]{2,1,0:T(8,128)(2,1)}, u32[]{:S(2)}, u32[]{:S(2)}) collective-permute-start(bf16[4,128,2048]{2,1,0:T(8,128)(2,1)} %own_ref.3), channel_id=1, source_target_pairs={{0,16},{16,32},{32,48},{48,64},{64,80},{80,96},{96,112},{112,128},... | collective-permute-start | bytes 6291464 | tf_op jit(solution)/shard_map/ppermute | solution.py:23
  9.1 9.0 %collective-permute-start.4 = (bf16[64,1024]{1,0:T(8,128)(2,1)}, bf16[64,1024]{1,0:T(8,128)(2,1)S(1)}, u32[]{:S(2)}, u32[]{:S(2)}) collective-permute-start(bf16[64,1024]{1,0:T(8,128)(2,1)} %get-tuple-element.34.refs_2_), channel_id=1, source_target_pairs={{0,2},{1,15},{2,4},{3,1},{4,6},{5,3},{6,8},{7,5},{8,10},{9,7},{10,... | collective-permute-start | bytes 393224 | tf_op jit(solution)/shard_map/ppermute | solution.py:38
  11.0 8.5 %collective-permute-start.5 = (bf16[64,1024]{1,0:T(8,128)(2,1)}, bf16[64,1024]{1,0:T(8,128)(2,1)S(1)}, u32[]{:S(2)}, u32[]{:S(2)}) collective-permute-start(bf16[64,1024]{1,0:T(8,128)(2,1)} %get-tuple-element.35.refs_3_), channel_id=1, source_target_pairs={{0,2},{1,15},{2,4},{3,1},{4,6},{5,3},{6,8},{7,5},{8,10},{9,7},{10,... | collective-permute-start | bytes 393224 | tf_op jit(solution)/shard_map/ppermute | solution.py:38
  12.9 48.6 %collective-permute-start.3 = (bf16[128,1024]{1,0:T(8,128)(2,1)}, bf16[128,1024]{1,0:T(8,128)(2,1)}, u32[]{:S(2)}, u32[]{:S(2)}) collective-permute-start(bf16[128,1024]{1,0:T(8,128)(2,1)} %get-tuple-element.36), channel_id=1, source_target_pairs={{0,1},{1,0},{2,3},{3,2},{4,5},{5,4},{6,7},{7,6},{8,9},{9,8},{10,11... | collective-permute-start | bytes 786440 | tf_op jit(solution)/shard_map/ppermute | solution.py:28
  25.0 42.0 %collective-permute-start.12 = (bf16[64,1024]{1,0:T(8,128)(2,1)}, bf16[64,1024]{1,0:T(8,128)(2,1)}, u32[]{:S(2)}, u32[]{:S(2)}) collective-permute-start(bf16[64,1024]{1,0:T(8,128)(2,1)} %collective-permute-done.8.refs_10_), channel_id=1, source_target_pairs={{0,2},{1,15},{2,4},{3,1},{4,6},{5,3},{6,8},{7,5},{8,10},{9,7},{10,... | collective-permute-start | bytes 393224 | tf_op jit(solution)/shard_map/ppermute | solution.py:38
  26.4 42.5 %collective-permute-start.13 = (bf16[64,1024]{1,0:T(8,128)(2,1)}, bf16[64,1024]{1,0:T(8,128)(2,1)}, u32[]{:S(2)}, u32[]{:S(2)}) collective-permute-start(bf16[64,1024]{1,0:T(8,128)(2,1)} %collective-permute-done.9.refs_11_), channel_id=1, source_target_pairs={{0,2},{1,15},{2,4},{3,1},{4,6},{5,3},{6,8},{7,5},{8,10},{9,7},{10,... | collective-permute-start | bytes 393224 | tf_op jit(solution)/shard_map/ppermute | solution.py:38
  61.5 55.9 %collective-permute-start.32 = (bf16[4,64,2048]{2,1,0:T(8,128)(2,1)}, bf16[4,64,2048]{2,1,0:T(8,128)(2,1)}, u32[]{:S(2)}, u32[]{:S(2)}) collective-permute-start(bf16[4,64,2048]{2,1,0:T(8,128)(2,1)} %get-tuple-element.38), channel_id=1, source_target_pairs={{0,1},{1,0},{2,3},{3,2},{4,5},{5,4},{6,7},{7,6},{8,9},{9,8},{10,11... | collective-permute-start | bytes 3145736 | tf_op jit(solution)/shard_map/ppermute | solution.py:28
  63.2 13.8 %collective-permute-start.7 = (bf16[64,1024]{1,0:T(8,128)(2,1)}, bf16[64,1024]{1,0:T(8,128)(2,1)}, u32[]{:S(2)}, u32[]{:S(2)}) collective-permute-start(bf16[64,1024]{1,0:T(8,128)(2,1)} %get-tuple-element.59.refs_5_), channel_id=1, source_target_pairs={{0,2},{1,15},{2,4},{3,1},{4,6},{5,3},{6,8},{7,5},{8,10},{9,7},{10,... | collective-permute-start | bytes 393224 | tf_op jit(solution)/shard_map/ppermute | solution.py:38
  65.1 11.9 %collective-permute-start.6 = (bf16[64,1024]{1,0:T(8,128)(2,1)}, bf16[64,1024]{1,0:T(8,128)(2,1)}, u32[]{:S(2)}, u32[]{:S(2)}) collective-permute-start(bf16[64,1024]{1,0:T(8,128)(2,1)} %get-tuple-element.60.refs_4_), channel_id=1, source_target_pairs={{0,2},{1,15},{2,4},{3,1},{4,6},{5,3},{6,8},{7,5},{8,10},{9,7},{10,... | collective-permute-start | bytes 393224 | tf_op jit(solution)/shard_map/ppermute | solution.py:38
  67.0 11.1 %collective-permute-start.16 = (bf16[64,1024]{1,0:T(8,128)(2,1)}, bf16[64,1024]{1,0:T(8,128)(2,1)}, u32[]{:S(2)}, u32[]{:S(2)}) collective-permute-start(bf16[64,1024]{1,0:T(8,128)(2,1)} %collective-permute-done.12.refs_14_), channel_id=1, source_target_pairs={{0,2},{1,15},{2,4},{3,1},{4,6},{5,3},{6,8},{7,5},{8,10},{9,7},{10,... | collective-permute-start | bytes 393224 | tf_op jit(solution)/shard_map/ppermute | solution.py:38
  68.9 10.2 %collective-permute-start.17 = (bf16[64,1024]{1,0:T(8,128)(2,1)}, bf16[64,1024]{1,0:T(8,128)(2,1)}, u32[]{:S(2)}, u32[]{:S(2)}) collective-permute-start(bf16[64,1024]{1,0:T(8,128)(2,1)} %collective-permute-done.13.refs_15_), channel_id=1, source_target_pairs={{0,2},{1,15},{2,4},{3,1},{4,6},{5,3},{6,8},{7,5},{8,10},{9,7},{10,... | collective-permute-start | bytes 393224 | tf_op jit(solution)/shard_map/ppermute | solution.py:38
  77.0 48.4 %collective-permute-start.2 = (bf16[4,64,2048]{2,1,0:T(8,128)(2,1)}, bf16[4,64,2048]{2,1,0:T(8,128)(2,1)}, u32[]{:S(2)}, u32[]{:S(2)}) collective-permute-start(bf16[4,64,2048]{2,1,0:T(8,128)(2,1)} %get-tuple-element.33), channel_id=1, source_target_pairs={{0,1},{1,0},{2,3},{3,2},{4,5},{5,4},{6,7},{7,6},{8,9},{9,8},{10,11... | collective-permute-start | bytes 3145736 | tf_op jit(solution)/shard_map/ppermute | solution.py:28
  79.1 7.2 %collective-permute-start.20 = (bf16[64,1024]{1,0:T(8,128)(2,1)}, bf16[64,1024]{1,0:T(8,128)(2,1)S(1)}, u32[]{:S(2)}, u32[]{:S(2)}) collective-permute-start(bf16[64,1024]{1,0:T(8,128)(2,1)} %collective-permute-done.16.refs_18_), channel_id=1, source_target_pairs={{0,2},{1,15},{2,4},{3,1},{4,6},{5,3},{6,8},{7,5},{8,10},{9,7},{10,... | collective-permute-start | bytes 393224 | tf_op jit(solution)/shard_map/ppermute | solution.py:38
  132.6 45.6 %collective-permute-start.33 = (bf16[4,128,1024]{2,1,0:T(8,128)(2,1)}, bf16[4,128,1024]{2,1,0:T(8,128)(2,1)}, u32[]{:S(2)}, u32[]{:S(2)}) collective-permute-start(bf16[4,128,1024]{2,1,0:T(8,128)(2,1)} %get-tuple-element.48), channel_id=1, source_target_pairs={{0,1},{1,0},{2,3},{3,2},{4,5},{5,4},{6,7},{7,6},{8,9},{9,8},{10,11... | collective-permute-start | bytes 3145736 | tf_op jit(solution)/shard_map/ppermute | solution.py:28
  132.7 14.5 %collective-permute-start.39 = (bf16[1,2,2,128,128]{4,3,2,1,0:T(8,128)(2,1)}, bf16[1,2,2,128,128]{4,3,2,1,0:T(8,128)(2,1)}, u32[]{:S(2)}, u32[]{:S(2)}) collective-permute-start(bf16[1,2,2,128,128]{4,3,2,1,0:T(8,128)(2,1)} %get-tuple-element.55), channel_id=1, source_target_pairs={{0,8},{1,9},{2,10},{3,11},{4,12},{5,13},{6,14},{7,15},{8,0},{9,1},... | collective-permute-start | bytes 393224 | tf_op jit(solution)/shard_map/ppermute | solution.py:38
  134.3 37.3 %collective-permute-start.42 = (bf16[2,2,2,128,128]{4,3,2,1,0:T(8,128)(2,1)}, bf16[2,2,2,128,128]{4,3,2,1,0:T(8,128)(2,1)}, u32[]{:S(2)}, u32[]{:S(2)}) collective-permute-start(bf16[2,2,2,128,128]{4,3,2,1,0:T(8,128)(2,1)} %get-tuple-element.58), channel_id=1, source_target_pairs={{0,10},{1,7},{2,12},{3,9},{4,14},{5,11},{6,0},{7,13},{8,2},{9,15},... | collective-permute-start | bytes 786440 | tf_op jit(solution)/shard_map/ppermute | solution.py:38
  136.1 17.8 %collective-permute-start.41 = (bf16[1,2,2,128,128]{4,3,2,1,0:T(8,128)(2,1)}, bf16[1,2,2,128,128]{4,3,2,1,0:T(8,128)(2,1)}, u32[]{:S(2)}, u32[]{:S(2)}) collective-permute-start(bf16[1,2,2,128,128]{4,3,2,1,0:T(8,128)(2,1)} %get-tuple-element.57), channel_id=1, source_target_pairs={{0,6},{1,11},{2,8},{3,13},{4,10},{5,15},{6,12},{7,1},{8,14},{9,3},... | collective-permute-start | bytes 393224 | tf_op jit(solution)/shard_map/ppermute | solution.py:38
  138.1 25.2 %collective-permute-start.38 = (bf16[1,2,2,128,128]{4,3,2,1,0:T(8,128)(2,1)}, bf16[1,2,2,128,128]{4,3,2,1,0:T(8,128)(2,1)}, u32[]{:S(2)}, u32[]{:S(2)}) collective-permute-start(bf16[1,2,2,128,128]{4,3,2,1,0:T(8,128)(2,1)} %get-tuple-element.54), channel_id=1, source_target_pairs={{0,8},{1,9},{2,10},{3,11},{4,12},{5,13},{6,14},{7,15},{8,0},{9,1},... | collective-permute-start | bytes 393224 | tf_op jit(solution)/shard_map/ppermute | solution.py:38
  147.3 24.4 %collective-permute-start.40 = (bf16[1,2,2,128,128]{4,3,2,1,0:T(8,128)(2,1)}, bf16[1,2,2,128,128]{4,3,2,1,0:T(8,128)(2,1)}, u32[]{:S(2)}, u32[]{:S(2)}) collective-permute-start(bf16[1,2,2,128,128]{4,3,2,1,0:T(8,128)(2,1)} %get-tuple-element.56), channel_id=1, source_target_pairs={{0,6},{1,11},{2,8},{3,13},{4,10},{5,15},{6,12},{7,1},{8,14},{9,3},... | collective-permute-start | bytes 393224 | tf_op jit(solution)/shard_map/ppermute | solution.py:38
  153.9 30.3 %collective-permute-start.34 = (bf16[2,2,2,128,128]{4,3,2,1,0:T(8,128)(2,1)}, bf16[2,2,2,128,128]{4,3,2,1,0:T(8,128)(2,1)}, u32[]{:S(2)}, u32[]{:S(2)}) collective-permute-start(bf16[2,2,2,128,128]{4,3,2,1,0:T(8,128)(2,1)} %get-tuple-element.49), channel_id=1, source_target_pairs={{0,4},{1,13},{2,6},{3,15},{4,8},{5,1},{6,10},{7,3},{8,12},{9,5},{1... | collective-permute-start | bytes 786440 | tf_op jit(solution)/shard_map/ppermute | solution.py:38
  163.3 20.9 %collective-permute-start.35 = (bf16[2,2,2,128,128]{4,3,2,1,0:T(8,128)(2,1)}, bf16[2,2,2,128,128]{4,3,2,1,0:T(8,128)(2,1)}, u32[]{:S(2)}, u32[]{:S(2)}) collective-permute-start(bf16[2,2,2,128,128]{4,3,2,1,0:T(8,128)(2,1)} %get-tuple-element.50), channel_id=1, source_target_pairs={{0,12},{1,5},{2,14},{3,7},{4,0},{5,9},{6,2},{7,11},{8,4},{9,13},{1... | collective-permute-start | bytes 786440 | tf_op jit(solution)/shard_map/ppermute | solution.py:38
  171.6 12.6 %collective-permute-start.36 = (bf16[2,2,2,128,128]{4,3,2,1,0:T(8,128)(2,1)}, bf16[2,2,2,128,128]{4,3,2,1,0:T(8,128)(2,1)}, u32[]{:S(2)}, u32[]{:S(2)}) collective-permute-start(bf16[2,2,2,128,128]{4,3,2,1,0:T(8,128)(2,1)} %get-tuple-element.51), channel_id=1, source_target_pairs={{0,2},{1,15},{2,4},{3,1},{4,6},{5,3},{6,8},{7,5},{8,10},{9,7},{10,... | collective-permute-start | bytes 786440 | tf_op jit(solution)/shard_map/ppermute | solution.py:38
  171.6 12.6 %collective-permute-start.37 = (bf16[2,2,2,128,128]{4,3,2,1,0:T(8,128)(2,1)}, bf16[2,2,2,128,128]{4,3,2,1,0:T(8,128)(2,1)}, u32[]{:S(2)}, u32[]{:S(2)}) collective-permute-start(bf16[2,2,2,128,128]{4,3,2,1,0:T(8,128)(2,1)} %get-tuple-element.52), channel_id=1, source_target_pairs={{0,14},{1,3},{2,0},{3,5},{4,2},{5,7},{6,4},{7,9},{8,6},{9,11},{10,... | collective-permute-start | bytes 786440 | tf_op jit(solution)/shard_map/ppermute | solution.py:38
  (39 other events, 252.2 us)

commit v2 on v1

--- a/solution.py
+++ b/solution.py
@@ -13,7 +13,7 @@
 PARTS = 2
 STREAMS = 4
 EARLY = (3, 4)
-LATE = (5, 2, 6, 1, 7)
+LATE = (5, 1, 7, 2, 6)
 FINISH = ((0, 4, 3, 5), (2, 6, 1, 7))
 
 
@@ -57,29 +57,34 @@
     chips = width // TILE // 2
     step = 32
 
-    def one_tile(t, carry):
-        source = pl.ds(pl.multiple_of(t * TILE, TILE), TILE)
-        targets = []
-        for turn in range(2):
-            dz = steps_from(t // 2, chips, turn)
-            dc = lax.rem(t + place()[1] + turn, 2)
-            targets.append(pl.ds(pl.multiple_of((dz * 2 + dc) * TILE, TILE), TILE))
+    def two_tiles(u, carry):
+        sources, targets = [], []
+        for i in range(2):
+            t = 2 * u + i
+            sources.append(pl.ds(pl.multiple_of(t * TILE, TILE), TILE))
+            for turn in range(2):
+                dz = steps_from(u, chips, turn)
+                dc = lax.rem(i + place()[1] + turn, 2)
+                targets.append(pl.ds(pl.multiple_of((dz * 2 + dc) * TILE, TILE), TILE))
         for start in range(0, rows, step):
-            total = [None] * pairs
+            total = [[None, None] for _ in range(pairs)]
             for q in range(3 * pairs):
                 ref = (before_ref, own_ref, after_ref)[q // pairs]
-                value = ref[q % pairs, start : start + step, source].astype(jnp.float32)
+                values = [ref[q % pairs, start : start + step, at].astype(jnp.float32) for at in sources]
                 for p in range(pairs):
                     if 0 <= q - p < taps:
-                        term = coef_ref[q - p, first + p] * value
-                        total[p] = term if total[p] is None else total[p] + term
+                        weight = coef_ref[q - p, first + p]
+                        for i in range(2):
+                            term = weight * values[i]
+                            total[p][i] = term if total[p][i] is None else total[p][i] + term
             for p in range(pairs):
-                rounded = total[p].astype(jnp.bfloat16)
-                for ref, target in zip(mixed_refs, targets):
-                    ref[p, start : start + step, target] = rounded
+                for i in range(2):
+                    rounded = total[p][i].astype(jnp.bfloat16)
+                    for turn in range(2):
+                        mixed_refs[turn][p, start : start + step, targets[2 * i + turn]] = rounded
         return carry
 
-    lax.fori_loop(0, width // TILE, one_tile, 0)
+    lax.fori_loop(0, width // TILE // 2, two_tiles, 0)
 
 
 def mix(which, coef, before, own, after):

time: 191 us -> 190 us (level)
  no operation moved by 1% of the time
where the time goes in v2:
time: 190 us; the launch traced here: 189 us
  waiting for transfers between devices  105 us (55%)
  starting transfers between devices  40 us (21%)
  Pallas kernels  37.1 us (20%)
  local copies, waits for them, and re-layouts  5.87 us (3%)
    ppermute x37, waiting for transfers between devices, mirrored(): return lax.ppermute(block, 'perm', route)  74.6 us
    ppermute x37, starting transfers between devices, mirrored(): return lax.ppermute(block, 'perm', route)  30.7 us
    ppermute x2, waiting for transfers between devices, wide_shift(): return lax.ppermute(block, 'wide', route)  30.2 us
    pallas_call x2, Pallas kernels, product(): pl.pallas_call(functools.partial(product_body, len(pieces), chips), out_s...  14.5 us
    pallas_call x2, Pallas kernels, finish(): pl.pallas_call(functools.partial(finish_body, splits), out_shape=jax.Shap...  11.8 us
    pallas_call x2, Pallas kernels, mix(): pl.pallas_call(mix_body, out_shape=[jax.ShapeDtypeStruct((pairs, rows, wi...  8.77 us
    ppermute x2, starting transfers between devices, wide_shift(): return lax.ppermute(block, 'wide', route)  7.1 us
  transfers between devices with their start and end apart: 43, of which 28 were waited for; matrix products, arithmetic and copies ran while one was open for 3% of the time, Pallas kernels for 13%

profile of v2, /device:TPU:6, one launch (start us, length us, event | category | flops | bytes accessed | tf_op | source)
XLA Modules:
  0.0 189.2 jit_solution(814405770924975870)
XLA Ops:
  0.0 5.2 %collective-permute-start.1 = (bf16[4,128,2048]{2,1,0:T(8,128)(2,1)}, bf16[4,128,2048]{2,1,0:T(8,128)(2,1)}, u32[]{:S(2)}, u32[]{:S(2)}) collective-permute-start(bf16[4,128,2048]{2,1,0:T(8,128)(2,1)} %own_ref.3), channel_id=1, source_target_pairs={{16,0},{32,16},{48,32},{64,48},{80,64},{96,80},{112,96},{128,112},... | collective-permute-start | bytes 6291464 | tf_op jit(solution)/shard_map/ppermute | solution.py:23
  14.9 3.2 %collective-permute-done.4.refs_6_ = bf16[64,1024]{1,0:T(8,128)(2,1)S(1)} collective-permute-done((bf16[64,1024]{1,0:T(8,128)(2,1)}, bf16[64,1024]{1,0:T(8,128)(2,1)S(1)}, u32[]{:S(2)}, u32[]{:S(2)}) %collective-permute-start.4) | collective-permute-done | bytes 131104 | tf_op jit(solution)/shard_map/ppermute | solution.py:38
  19.5 5.5 %collective-permute-done.8.refs_10_ = bf16[64,1024]{1,0:T(8,128)(2,1)} collective-permute-done((bf16[64,1024]{1,0:T(8,128)(2,1)S(1)}, bf16[64,1024]{1,0:T(8,128)(2,1)}, u32[]{:S(2)}, u32[]{:S(2)}) %collective-permute-start.8) | collective-permute-done | bytes 131104 | tf_op jit(solution)/shard_map/ppermute | solution.py:38
  26.4 23.9 %collective-permute-done.1.after_ref = bf16[4,128,2048]{2,1,0:T(8,128)(2,1)} collective-permute-done((bf16[4,128,2048]{2,1,0:T(8,128)(2,1)}, bf16[4,128,2048]{2,1,0:T(8,128)(2,1)}, u32[]{:S(2)}, u32[]{:S(2)}) %collective-permute-start.1) | collective-permute-done | bytes 2097184 | tf_op jit(solution)/shard_map/ppermute | solution.py:23
  50.4 6.2 %collective-permute-done.before_ref = bf16[4,128,2048]{2,1,0:T(8,128)(2,1)} collective-permute-done((bf16[4,128,2048]{2,1,0:T(8,128)(2,1)}, bf16[4,128,2048]{2,1,0:T(8,128)(2,1)}, u32[]{:S(2)}, u32[]{:S(2)}) %collective-permute-start) | collective-permute-done | bytes 2097184 | tf_op jit(solution)/shard_map/ppermute | solution.py:23
  56.6 4.4 %mix.3 = (bf16[4,64,2048]{2,1,0:T(8,128)(2,1)}, bf16[4,64,2048]{2,1,0:T(8,128)(2,1)}) custom-call(f32[9,64]{1,0:T(8,128)} %bitcast.8, bf16[4,128,2048]{2,1,0:T(8,128)(2,1)} %collective-permute-done.before_ref, bf16[4,128,2048]{2,1,0:T(8,128)(2,1)} %own_ref.3, bf16[4,128,2048]{2,1,0:T(8,128)(2,1)} %collective-permute-done.1.after_ref), custom_call_target="tpu_custom_call" | custom-call | flops 9437184 | bytes 4194304 | tf_op jit(solution)/shard_map/mix/pallas_call | solution.py:97
  68.4 3.1 %collective-permute-start.17 = (bf16[64,1024]{1,0:T(8,128)(2,1)}, bf16[64,1024]{1,0:T(8,128)(2,1)}, u32[]{:S(2)}, u32[]{:S(2)}) collective-permute-start(bf16[64,1024]{1,0:T(8,128)(2,1)} %collective-permute-done.13.refs_15_), channel_id=1, source_target_pairs={{0,2},{1,15},{2,4},{3,1},{4,6},{5,3},{6,8},{7,5},{8,10},{9,7},{10,... | collective-permute-start | bytes 393224 | tf_op jit(solution)/shard_map/ppermute | solution.py:38
  71.6 4.4 %mix.2 = (bf16[4,64,2048]{2,1,0:T(8,128)(2,1)}, bf16[4,64,2048]{2,1,0:T(8,128)(2,1)}) custom-call(f32[9,64]{1,0:T(8,128)} %bitcast.9, bf16[4,128,2048]{2,1,0:T(8,128)(2,1)} %collective-permute-done.before_ref, bf16[4,128,2048]{2,1,0:T(8,128)(2,1)} %own_ref.3, bf16[4,128,2048]{2,1,0:T(8,128)(2,1)} %collective-permute-done.1.after_ref), custom_call_target="tpu_custom_call" | custom-call | flops 9437184 | bytes 4194304 | tf_op jit(solution)/shard_map/mix/pallas_call | solution.py:97
  79.2 3.3 %collective-permute-done.11.refs_13_ = bf16[64,1024]{1,0:T(8,128)(2,1)S(1)} collective-permute-done((bf16[64,1024]{1,0:T(8,128)(2,1)}, bf16[64,1024]{1,0:T(8,128)(2,1)S(1)}, u32[]{:S(2)}, u32[]{:S(2)}) %collective-permute-start.11) | collective-permute-done | bytes 131104 | tf_op jit(solution)/shard_map/ppermute | solution.py:38
  85.3 3.6 %collective-permute-done.21.refs_23_ = bf16[64,1024]{1,0:T(8,128)(2,1)S(1)} collective-permute-done((bf16[64,1024]{1,0:T(8,128)(2,1)}, bf16[64,1024]{1,0:T(8,128)(2,1)S(1)}, u32[]{:S(2)}, u32[]{:S(2)}) %collective-permute-start.21) | collective-permute-done | bytes 131104 | tf_op jit(solution)/shard_map/ppermute | solution.py:38
  91.7 3.4 %collective-permute-done.24.refs_26_ = bf16[64,1024]{1,0:T(8,128)(2,1)S(1)} collective-permute-done((bf16[64,1024]{1,0:T(8,128)(2,1)S(1)}, bf16[64,1024]{1,0:T(8,128)(2,1)S(1)}, u32[]{:S(2)}, u32[]{:S(2)}) %collective-permute-start.24) | collective-permute-done | bytes 131104 | tf_op jit(solution)/shard_map/ppermute | solution.py:38
  97.9 3.4 %collective-permute-done.25.refs_27_ = bf16[64,1024]{1,0:T(8,128)(2,1)S(1)} collective-permute-done((bf16[64,1024]{1,0:T(8,128)(2,1)S(1)}, bf16[64,1024]{1,0:T(8,128)(2,1)S(1)}, u32[]{:S(2)}, u32[]{:S(2)}) %collective-permute-start.25) | collective-permute-done | bytes 131104 | tf_op jit(solution)/shard_map/ppermute | solution.py:38
  104.0 3.4 %collective-permute-done.28.refs_30_ = bf16[64,1024]{1,0:T(8,128)(2,1)S(1)} collective-permute-done((bf16[64,1024]{1,0:T(8,128)(2,1)S(1)}, bf16[64,1024]{1,0:T(8,128)(2,1)S(1)}, u32[]{:S(2)}, u32[]{:S(2)}) %collective-permute-start.28) | collective-permute-done | bytes 131104 | tf_op jit(solution)/shard_map/ppermute | solution.py:38
  110.2 3.4 %collective-permute-done.29.refs_31_ = bf16[64,1024]{1,0:T(8,128)(2,1)S(1)} collective-permute-done((bf16[64,1024]{1,0:T(8,128)(2,1)S(1)}, bf16[64,1024]{1,0:T(8,128)(2,1)S(1)}, u32[]{:S(2)}, u32[]{:S(2)}) %collective-permute-start.29) | collective-permute-done | bytes 131104 | tf_op jit(solution)/shard_map/ppermute | solution.py:38
  117.1 7.3 %product.2 = (bf16[4,128,1024]{2,1,0:T(8,128)(2,1)}, bf16[4,128,1024]{2,1,0:T(8,128)(2,1)}, bf16[2,2,2,128,128]{4,3,2,1,0:T(8,128)(2,1)}, bf16[2,2,2,128,128]{4,...) custom-call(bf16[4,64,2048]{2,1,0:T(8,128)(2,1)} %get-tuple-element., ...), custom_call_target="tpu_custom_call" | custom-call | flops 2147483648 | bytes 7340032 | tf_op jit(solution)/shard_map/product/pallas_call | solution.py:187
  124.3 7.3 %product.3 = (bf16[4,128,1024]{2,1,0:T(8,128)(2,1)}, bf16[4,128,1024]{2,1,0:T(8,128)(2,1)}, bf16[2,2,2,128,128]{4,3,2,1,0:T(8,128)(2,1)}, bf16[2,2,2,128,128]{4,...) custom-call(bf16[4,64,2048]{2,1,0:T(8,128)(2,1)} %get-tuple-element., ...), custom_call_target="tpu_custom_call", output_to_operand_aliasing={{0}: (34, {}), {1}: (35, {}), {2}: (36, {}), {3}: (37, {}),... | custom-call | flops 2147483648 | bytes 7340032 | tf_op jit(solution)/shard_map/product/pallas_call | solution.py:187
  137.3 4.3 %collective-permute-start.38 = (bf16[1,2,2,128,128]{4,3,2,1,0:T(8,128)(2,1)}, bf16[1,2,2,128,128]{4,3,2,1,0:T(8,128)(2,1)}, u32[]{:S(2)}, u32[]{:S(2)}) collective-permute-start(bf16[1,2,2,128,128]{4,3,2,1,0:T(8,128)(2,1)} %get-tuple-element.54), channel_id=1, source_target_pairs={{0,8},{1,9},{2,10},{3,11},{4,12},{5,13},{6,14},{7,15},{8,0},{9,1},... | collective-permute-start | bytes 393224 | tf_op jit(solution)/shard_map/ppermute | solution.py:38
  141.6 4.7 %collective-permute-done.39.refs_2_ = bf16[1,2,2,128,128]{4,3,2,1,0:T(8,128)(2,1)} collective-permute-done((bf16[1,2,2,128,128]{4,3,2,1,0:T(8,128)(2,1)}, bf16[1,2,2,128,128]{4,3,2,1,0:T(8,128)(2,1)}, u32[]{:S(2)}, u32[]{:S(2)}) %collective-permute-start.39) | collective-permute-done | bytes 131104 | tf_op jit(solution)/shard_map/ppermute | solution.py:38
  148.7 4.0 %collective-permute-done.41.refs_4_ = bf16[1,2,2,128,128]{4,3,2,1,0:T(8,128)(2,1)} collective-permute-done((bf16[1,2,2,128,128]{4,3,2,1,0:T(8,128)(2,1)}, bf16[1,2,2,128,128]{4,3,2,1,0:T(8,128)(2,1)}, u32[]{:S(2)}, u32[]{:S(2)}) %collective-permute-start.41) | collective-permute-done | bytes 131104 | tf_op jit(solution)/shard_map/ppermute | solution.py:38
  152.7 9.7 %collective-permute-done.38.refs_1_ = bf16[1,2,2,128,128]{4,3,2,1,0:T(8,128)(2,1)} collective-permute-done((bf16[1,2,2,128,128]{4,3,2,1,0:T(8,128)(2,1)}, bf16[1,2,2,128,128]{4,3,2,1,0:T(8,128)(2,1)}, u32[]{:S(2)}, u32[]{:S(2)}) %collective-permute-start.38) | collective-permute-done | bytes 131104 | tf_op jit(solution)/shard_map/ppermute | solution.py:38
  162.4 8.3 %collective-permute-done.40.refs_3_ = bf16[1,2,2,128,128]{4,3,2,1,0:T(8,128)(2,1)} collective-permute-done((bf16[1,2,2,128,128]{4,3,2,1,0:T(8,128)(2,1)}, bf16[1,2,2,128,128]{4,3,2,1,0:T(8,128)(2,1)}, u32[]{:S(2)}, u32[]{:S(2)}) %collective-permute-start.40) | collective-permute-done | bytes 131104 | tf_op jit(solution)/shard_map/ppermute | solution.py:38
  170.7 3.2 %collective-permute-start.37 = (bf16[2,2,2,128,128]{4,3,2,1,0:T(8,128)(2,1)}, bf16[2,2,2,128,128]{4,3,2,1,0:T(8,128)(2,1)}, u32[]{:S(2)}, u32[]{:S(2)}) collective-permute-start(bf16[2,2,2,128,128]{4,3,2,1,0:T(8,128)(2,1)} %get-tuple-element.52), channel_id=1, source_target_pairs={{0,14},{1,3},{2,0},{3,5},{4,2},{5,7},{6,4},{7,9},{8,6},{9,11},{10,... | collective-permute-start | bytes 786440 | tf_op jit(solution)/shard_map/ppermute | solution.py:38
  177.4 5.9 %finish.2.refs_4_ = bf16[4,128,2048]{2,1,0:T(8,128)(2,1)} custom-call(s32[4]{0:T(128)} %get-tuple-element.61.source_ref, s32[16]{0:T(128)} %sizes_ref.3, f32[4]{0:T(128)} %pair_ref.3, s32[16,4]{1,0:T(8,128)} %bitcast.6, f32[128,1]{1,0:T(8,128)} %copy.21.row_ref, f32[16,1,128]{2,1,0:T(1,128)} %bitcast.10, bf16[4,128,1024]{2,1,0:T(8,128)(2,1)} %get-tuple-element.47.own_ref, ...), custom_call_target="tpu_custom_call" | custom-call | flops 5242880 | bytes 3145728 | tf_op jit(solution)/shard_map/finish/pallas_call | solution.py:258
  183.3 5.9 %finish.3 = bf16[4,128,2048]{2,1,0:T(8,128)(2,1)} custom-call(s32[4]{0:T(128)} %get-tuple-element.62.source_ref, s32[16]{0:T(128)} %sizes_ref.3, f32[4]{0:T(128)} %pair_ref.3, s32[16,4]{1,0:T(8,128)} %bitcast.7, f32[128,1]{1,0:T(8,128)} %copy.21.row_ref, f32[16,1,128]{2,1,0:T(1,128)} %bitcast.11, ...), custom_call_target="tpu_custom_call", output_to_operand_aliasing={{}: (12, {})} | custom-call | flops 5242880 | bytes 3145728 | tf_op jit(solution)/shard_map/finish/pallas_call | solution.py:258
  (115 shorter events, 52.2 us)
Async XLA Ops:
  0.0 50.4 %collective-permute-start.1 = (bf16[4,128,2048]{2,1,0:T(8,128)(2,1)}, bf16[4,128,2048]{2,1,0:T(8,128)(2,1)}, u32[]{:S(2)}, u32[]{:S(2)}) collective-permute-start(bf16[4,128,2048]{2,1,0:T(8,128)(2,1)} %own_ref.3), channel_id=1, source_target_pairs={{16,0},{32,16},{48,32},{64,48},{80,64},{96,80},{112,96},{128,112},... | collective-permute-start | bytes 6291464 | tf_op jit(solution)/shard_map/ppermute | solution.py:23
  5.2 51.4 %collective-permute-start = (bf16[4,128,2048]{2,1,0:T(8,128)(2,1)}, bf16[4,128,2048]{2,1,0:T(8,128)(2,1)}, u32[]{:S(2)}, u32[]{:S(2)}) collective-permute-start(bf16[4,128,2048]{2,1,0:T(8,128)(2,1)} %own_ref.3), channel_id=1, source_target_pairs={{0,16},{16,32},{32,48},{48,64},{64,80},{80,96},{96,112},{112,128},... | collective-permute-start | bytes 6291464 | tf_op jit(solution)/shard_map/ppermute | solution.py:23
  9.1 9.0 %collective-permute-start.4 = (bf16[64,1024]{1,0:T(8,128)(2,1)}, bf16[64,1024]{1,0:T(8,128)(2,1)S(1)}, u32[]{:S(2)}, u32[]{:S(2)}) collective-permute-start(bf16[64,1024]{1,0:T(8,128)(2,1)} %get-tuple-element.34.refs_2_), channel_id=1, source_target_pairs={{0,2},{1,15},{2,4},{3,1},{4,6},{5,3},{6,8},{7,5},{8,10},{9,7},{10,... | collective-permute-start | bytes 393224 | tf_op jit(solution)/shard_map/ppermute | solution.py:38
  11.0 8.5 %collective-permute-start.5 = (bf16[64,1024]{1,0:T(8,128)(2,1)}, bf16[64,1024]{1,0:T(8,128)(2,1)S(1)}, u32[]{:S(2)}, u32[]{:S(2)}) collective-permute-start(bf16[64,1024]{1,0:T(8,128)(2,1)} %get-tuple-element.35.refs_3_), channel_id=1, source_target_pairs={{0,2},{1,15},{2,4},{3,1},{4,6},{5,3},{6,8},{7,5},{8,10},{9,7},{10,... | collective-permute-start | bytes 393224 | tf_op jit(solution)/shard_map/ppermute | solution.py:38
  12.9 48.1 %collective-permute-start.3 = (bf16[128,1024]{1,0:T(8,128)(2,1)}, bf16[128,1024]{1,0:T(8,128)(2,1)}, u32[]{:S(2)}, u32[]{:S(2)}) collective-permute-start(bf16[128,1024]{1,0:T(8,128)(2,1)} %get-tuple-element.36), channel_id=1, source_target_pairs={{0,1},{1,0},{2,3},{3,2},{4,5},{5,4},{6,7},{7,6},{8,9},{9,8},{10,11... | collective-permute-start | bytes 786440 | tf_op jit(solution)/shard_map/ppermute | solution.py:28
  25.0 41.5 %collective-permute-start.12 = (bf16[64,1024]{1,0:T(8,128)(2,1)}, bf16[64,1024]{1,0:T(8,128)(2,1)}, u32[]{:S(2)}, u32[]{:S(2)}) collective-permute-start(bf16[64,1024]{1,0:T(8,128)(2,1)} %collective-permute-done.8.refs_10_), channel_id=1, source_target_pairs={{0,2},{1,15},{2,4},{3,1},{4,6},{5,3},{6,8},{7,5},{8,10},{9,7},{10,... | collective-permute-start | bytes 393224 | tf_op jit(solution)/shard_map/ppermute | solution.py:38
  26.4 42.0 %collective-permute-start.13 = (bf16[64,1024]{1,0:T(8,128)(2,1)}, bf16[64,1024]{1,0:T(8,128)(2,1)}, u32[]{:S(2)}, u32[]{:S(2)}) collective-permute-start(bf16[64,1024]{1,0:T(8,128)(2,1)} %collective-permute-done.9.refs_11_), channel_id=1, source_target_pairs={{0,2},{1,15},{2,4},{3,1},{4,6},{5,3},{6,8},{7,5},{8,10},{9,7},{10,... | collective-permute-start | bytes 393224 | tf_op jit(solution)/shard_map/ppermute | solution.py:38
  61.0 55.4 %collective-permute-start.32 = (bf16[4,64,2048]{2,1,0:T(8,128)(2,1)}, bf16[4,64,2048]{2,1,0:T(8,128)(2,1)}, u32[]{:S(2)}, u32[]{:S(2)}) collective-permute-start(bf16[4,64,2048]{2,1,0:T(8,128)(2,1)} %get-tuple-element.38), channel_id=1, source_target_pairs={{0,1},{1,0},{2,3},{3,2},{4,5},{5,4},{6,7},{7,6},{8,9},{9,8},{10,11... | collective-permute-start | bytes 3145736 | tf_op jit(solution)/shard_map/ppermute | solution.py:28
  62.7 13.3 %collective-permute-start.7 = (bf16[64,1024]{1,0:T(8,128)(2,1)}, bf16[64,1024]{1,0:T(8,128)(2,1)}, u32[]{:S(2)}, u32[]{:S(2)}) collective-permute-start(bf16[64,1024]{1,0:T(8,128)(2,1)} %get-tuple-element.59.refs_5_), channel_id=1, source_target_pairs={{0,2},{1,15},{2,4},{3,1},{4,6},{5,3},{6,8},{7,5},{8,10},{9,7},{10,... | collective-permute-start | bytes 393224 | tf_op jit(solution)/shard_map/ppermute | solution.py:38
  64.6 11.4 %collective-permute-start.6 = (bf16[64,1024]{1,0:T(8,128)(2,1)}, bf16[64,1024]{1,0:T(8,128)(2,1)}, u32[]{:S(2)}, u32[]{:S(2)}) collective-permute-start(bf16[64,1024]{1,0:T(8,128)(2,1)} %get-tuple-element.60.refs_4_), channel_id=1, source_target_pairs={{0,2},{1,15},{2,4},{3,1},{4,6},{5,3},{6,8},{7,5},{8,10},{9,7},{10,... | collective-permute-start | bytes 393224 | tf_op jit(solution)/shard_map/ppermute | solution.py:38
  66.5 10.6 %collective-permute-start.16 = (bf16[64,1024]{1,0:T(8,128)(2,1)}, bf16[64,1024]{1,0:T(8,128)(2,1)}, u32[]{:S(2)}, u32[]{:S(2)}) collective-permute-start(bf16[64,1024]{1,0:T(8,128)(2,1)} %collective-permute-done.12.refs_14_), channel_id=1, source_target_pairs={{0,2},{1,15},{2,4},{3,1},{4,6},{5,3},{6,8},{7,5},{8,10},{9,7},{10,... | collective-permute-start | bytes 393224 | tf_op jit(solution)/shard_map/ppermute | solution.py:38
  68.4 9.7 %collective-permute-start.17 = (bf16[64,1024]{1,0:T(8,128)(2,1)}, bf16[64,1024]{1,0:T(8,128)(2,1)}, u32[]{:S(2)}, u32[]{:S(2)}) collective-permute-start(bf16[64,1024]{1,0:T(8,128)(2,1)} %collective-permute-done.13.refs_15_), channel_id=1, source_target_pairs={{0,2},{1,15},{2,4},{3,1},{4,6},{5,3},{6,8},{7,5},{8,10},{9,7},{10,... | collective-permute-start | bytes 393224 | tf_op jit(solution)/shard_map/ppermute | solution.py:38
  76.0 48.4 %collective-permute-start.2 = (bf16[4,64,2048]{2,1,0:T(8,128)(2,1)}, bf16[4,64,2048]{2,1,0:T(8,128)(2,1)}, u32[]{:S(2)}, u32[]{:S(2)}) collective-permute-start(bf16[4,64,2048]{2,1,0:T(8,128)(2,1)} %get-tuple-element.33), channel_id=1, source_target_pairs={{0,1},{1,0},{2,3},{3,2},{4,5},{5,4},{6,7},{7,6},{8,9},{9,8},{10,11... | collective-permute-start | bytes 3145736 | tf_op jit(solution)/shard_map/ppermute | solution.py:28
  78.1 7.2 %collective-permute-start.20 = (bf16[64,1024]{1,0:T(8,128)(2,1)}, bf16[64,1024]{1,0:T(8,128)(2,1)S(1)}, u32[]{:S(2)}, u32[]{:S(2)}) collective-permute-start(bf16[64,1024]{1,0:T(8,128)(2,1)} %collective-permute-done.16.refs_18_), channel_id=1, source_target_pairs={{0,2},{1,15},{2,4},{3,1},{4,6},{5,3},{6,8},{7,5},{8,10},{9,7},{10,... | collective-permute-start | bytes 393224 | tf_op jit(solution)/shard_map/ppermute | solution.py:38
  131.6 45.7 %collective-permute-start.33 = (bf16[4,128,1024]{2,1,0:T(8,128)(2,1)}, bf16[4,128,1024]{2,1,0:T(8,128)(2,1)}, u32[]{:S(2)}, u32[]{:S(2)}) collective-permute-start(bf16[4,128,1024]{2,1,0:T(8,128)(2,1)} %get-tuple-element.48), channel_id=1, source_target_pairs={{0,1},{1,0},{2,3},{3,2},{4,5},{5,4},{6,7},{7,6},{8,9},{9,8},{10,11... | collective-permute-start | bytes 3145736 | tf_op jit(solution)/shard_map/ppermute | solution.py:28
  131.7 14.6 %collective-permute-start.39 = (bf16[1,2,2,128,128]{4,3,2,1,0:T(8,128)(2,1)}, bf16[1,2,2,128,128]{4,3,2,1,0:T(8,128)(2,1)}, u32[]{:S(2)}, u32[]{:S(2)}) collective-permute-start(bf16[1,2,2,128,128]{4,3,2,1,0:T(8,128)(2,1)} %get-tuple-element.55), channel_id=1, source_target_pairs={{0,8},{1,9},{2,10},{3,11},{4,12},{5,13},{6,14},{7,15},{8,0},{9,1},... | collective-permute-start | bytes 393224 | tf_op jit(solution)/shard_map/ppermute | solution.py:38
  133.5 37.2 %collective-permute-start.42 = (bf16[2,2,2,128,128]{4,3,2,1,0:T(8,128)(2,1)}, bf16[2,2,2,128,128]{4,3,2,1,0:T(8,128)(2,1)}, u32[]{:S(2)}, u32[]{:S(2)}) collective-permute-start(bf16[2,2,2,128,128]{4,3,2,1,0:T(8,128)(2,1)} %get-tuple-element.58), channel_id=1, source_target_pairs={{0,10},{1,7},{2,12},{3,9},{4,14},{5,11},{6,0},{7,13},{8,2},{9,15},... | collective-permute-start | bytes 786440 | tf_op jit(solution)/shard_map/ppermute | solution.py:38
  135.1 17.6 %collective-permute-start.41 = (bf16[1,2,2,128,128]{4,3,2,1,0:T(8,128)(2,1)}, bf16[1,2,2,128,128]{4,3,2,1,0:T(8,128)(2,1)}, u32[]{:S(2)}, u32[]{:S(2)}) collective-permute-start(bf16[1,2,2,128,128]{4,3,2,1,0:T(8,128)(2,1)} %get-tuple-element.57), channel_id=1, source_target_pairs={{0,6},{1,11},{2,8},{3,13},{4,10},{5,15},{6,12},{7,1},{8,14},{9,3},... | collective-permute-start | bytes 393224 | tf_op jit(solution)/shard_map/ppermute | solution.py:38
  137.3 25.1 %collective-permute-start.38 = (bf16[1,2,2,128,128]{4,3,2,1,0:T(8,128)(2,1)}, bf16[1,2,2,128,128]{4,3,2,1,0:T(8,128)(2,1)}, u32[]{:S(2)}, u32[]{:S(2)}) collective-permute-start(bf16[1,2,2,128,128]{4,3,2,1,0:T(8,128)(2,1)} %get-tuple-element.54), channel_id=1, source_target_pairs={{0,8},{1,9},{2,10},{3,11},{4,12},{5,13},{6,14},{7,15},{8,0},{9,1},... | collective-permute-start | bytes 393224 | tf_op jit(solution)/shard_map/ppermute | solution.py:38
  146.3 24.4 %collective-permute-start.40 = (bf16[1,2,2,128,128]{4,3,2,1,0:T(8,128)(2,1)}, bf16[1,2,2,128,128]{4,3,2,1,0:T(8,128)(2,1)}, u32[]{:S(2)}, u32[]{:S(2)}) collective-permute-start(bf16[1,2,2,128,128]{4,3,2,1,0:T(8,128)(2,1)} %get-tuple-element.56), channel_id=1, source_target_pairs={{0,6},{1,11},{2,8},{3,13},{4,10},{5,15},{6,12},{7,1},{8,14},{9,3},... | collective-permute-start | bytes 393224 | tf_op jit(solution)/shard_map/ppermute | solution.py:38
  152.7 30.5 %collective-permute-start.34 = (bf16[2,2,2,128,128]{4,3,2,1,0:T(8,128)(2,1)}, bf16[2,2,2,128,128]{4,3,2,1,0:T(8,128)(2,1)}, u32[]{:S(2)}, u32[]{:S(2)}) collective-permute-start(bf16[2,2,2,128,128]{4,3,2,1,0:T(8,128)(2,1)} %get-tuple-element.49), channel_id=1, source_target_pairs={{0,4},{1,13},{2,6},{3,15},{4,8},{5,1},{6,10},{7,3},{8,12},{9,5},{1... | collective-permute-start | bytes 786440 | tf_op jit(solution)/shard_map/ppermute | solution.py:38
  162.4 20.8 %collective-permute-start.35 = (bf16[2,2,2,128,128]{4,3,2,1,0:T(8,128)(2,1)}, bf16[2,2,2,128,128]{4,3,2,1,0:T(8,128)(2,1)}, u32[]{:S(2)}, u32[]{:S(2)}) collective-permute-start(bf16[2,2,2,128,128]{4,3,2,1,0:T(8,128)(2,1)} %get-tuple-element.50), channel_id=1, source_target_pairs={{0,12},{1,5},{2,14},{3,7},{4,0},{5,9},{6,2},{7,11},{8,4},{9,13},{1... | collective-permute-start | bytes 786440 | tf_op jit(solution)/shard_map/ppermute | solution.py:38
  170.7 12.6 %collective-permute-start.36 = (bf16[2,2,2,128,128]{4,3,2,1,0:T(8,128)(2,1)}, bf16[2,2,2,128,128]{4,3,2,1,0:T(8,128)(2,1)}, u32[]{:S(2)}, u32[]{:S(2)}) collective-permute-start(bf16[2,2,2,128,128]{4,3,2,1,0:T(8,128)(2,1)} %get-tuple-element.51), channel_id=1, source_target_pairs={{0,2},{1,15},{2,4},{3,1},{4,6},{5,3},{6,8},{7,5},{8,10},{9,7},{10,... | collective-permute-start | bytes 786440 | tf_op jit(solution)/shard_map/ppermute | solution.py:38
  170.7 12.6 %collective-permute-start.37 = (bf16[2,2,2,128,128]{4,3,2,1,0:T(8,128)(2,1)}, bf16[2,2,2,128,128]{4,3,2,1,0:T(8,128)(2,1)}, u32[]{:S(2)}, u32[]{:S(2)}) collective-permute-start(bf16[2,2,2,128,128]{4,3,2,1,0:T(8,128)(2,1)} %get-tuple-element.52), channel_id=1, source_target_pairs={{0,14},{1,3},{2,0},{3,5},{4,2},{5,7},{6,4},{7,9},{8,6},{9,11},{10,... | collective-permute-start | bytes 786440 | tf_op jit(solution)/shard_map/ppermute | solution.py:38
  (39 other events, 252.2 us)
